TPU v7x, 256 devices: a whole 4x4x8 slice. The times are simulated.
256 devices in a mesh: blk: 8 (over y, x_hi), ctx: 32 (over z, x_lo, core).
Axes of the slice: x: 4 (x_hi: 2, x_lo: 2; x = x_hi * 2 + x_lo), y: 4, z: 8, core: 2. Of those that a mesh axis runs over, the one named last changes fastest.
Arguments:
- tokens: bfloat16 [8, 4096, 1024], P('blk', 'ctx'), may hold values from -16 to 16
- segment_ids: int32 [8, 4096], P('blk', 'ctx'), may hold values from 0 to 3, never falling along the last dimension, each value on 1 to 3072 neighbouring positions
- norm_gain: bfloat16 [8, 2, 1024], P('blk'), may hold values from 0.25 to 1.75
- w_mamba_in: bfloat16 [8, 1024, 2048], P('blk', None, 'ctx'), may hold values from -0.1875 to 0.1875
- w_ssm_param: bfloat16 [8, 1024, 160], P('blk'), may hold values from -0.1875 to 0.1875
- ssm_rate: bfloat16 [8, 32], P('blk'), may hold values from 7.2956085e-05 to 0.059814453
- dt_bias: bfloat16 [8, 32], P('blk'), may hold values from -1 to 1
- skip_gain: bfloat16 [8, 32], P('blk'), may hold values from 0.5 to 1.5
- ssm_norm_gain: bfloat16 [8, 2048], P('blk'), may hold values from 0.25 to 1.75
- w_mamba_out: bfloat16 [8, 2048, 1024], P('blk', 'ctx'), may hold values from -0.125 to 0.125
- w_qkv: bfloat16 [8, 1024, 2048], P('blk', None, 'ctx'), may hold values from -1.5 to 1.5
- w_attn_out: bfloat16 [8, 1024, 1024], P('blk', 'ctx'), may hold values from -0.75 to 0.75
Outputs:
- layer_out: bfloat16 [8, 4096, 1024], P('blk', 'ctx')
Inputs may be any that keep to these rules, and one draw needn't show every extreme that they name: `segment_ids`: within each micro-batch the ids never fall along the sequence; each document holds 1 to 3072 tokens, and one holds exactly that many.
All inputs are finite; a program needn't handle non-finite values.
Results may differ from a plain program's by a relative error of at most 0.015.
Values may be sent and summed in bfloat16 or wider, within the bound.
No kernel may reach another device: no remote copies, remote signals or barrier semaphores. Data moves between devices by JAX's collectives and lax.ppermute only.
A program may use at most 128 MiB of HBM per device.

v0:
```python
import math

import jax
import jax.numpy as jnp
from jax import lax
from jax.sharding import Mesh
from jax.sharding import PartitionSpec as P

INNER = 2048
HEAD_DIM = 64
STATE = 64
QUERY_HEADS = 8
KV_HEADS = 4
ATTN_DIM = 128
SPAN = 64
CTX = ("ctx_0", "ctx_1", "ctx_2")


epsilon = 1e-05
highest = lax.Precision.HIGHEST


def filled_with(value, identity):
    return jax.tree.map(
        lambda part, zero: jnp.zeros_like(part) + jnp.asarray(zero, part.dtype), value, identity
    )


def gathered_once(value, axis):
    leaves = jax.tree.leaves(value)
    turns = sorted(range(len(leaves)), key=lambda k: -leaves[k].size)
    width = (1, *leaves[turns[0]].shape)[-1]
    lines = [
        jnp.pad(leaves[k].reshape(-1), (0, -leaves[k].size % width)).reshape(-1, width)
        for k in turns
    ]
    both, at, found = (lax.all_gather(jnp.concatenate(lines), axis), 0, {})
    for k, line in zip(turns, lines):
        slab = both[:, at : at + len(line)].reshape(len(both), -1)
        found[k] = slab[:, : leaves[k].size].reshape(-1, *leaves[k].shape)
        at += len(line)
    numbers = iter(range(len(leaves)))
    return jax.tree.map(lambda _: found[next(numbers)], value)


def collected_alike(value, axis):
    leaves, found = (jax.tree.leaves(value), {})
    for initial, a in enumerate(leaves):
        if initial not in found:
            alike = [k for k, b in enumerate(leaves) if b.dtype == a.dtype]
            got = (
                gathered_once([leaves[k] for k in alike], axis)
                if len(alike) > 1
                else [lax.all_gather(a, axis)]
            )
            for k, b in zip(alike, got):
                found[k] = b
    numbers = iter(range(len(leaves)))
    return jax.tree.map(lambda _: found[next(numbers)], value)


def entering_2(value, axes, combine, identity):
    before = start = filled_with(value, identity)
    so_far = value
    for axis in reversed(axes):
        size, mine = (lax.axis_size(axis), lax.axis_index(axis))
        pieces = collected_alike(so_far, axis)
        inside, so_far = (start, start)
        for k in range(size):
            passed = k < mine
            so_far = combine(so_far, jax.tree.map(lambda part: part[k], pieces))
            inside = jax.tree.map(lambda new, old: jnp.where(passed, new, old), so_far, inside)
        before = combine(inside, before)
    return before


def joined_along(blocks, dim):
    dims = list(blocks.shape[1:])
    dims[dim] *= blocks.shape[0]
    return jnp.moveaxis(blocks, 0, dim).reshape(dims)


def all_blocks(value, axes, turns):
    blocks = value
    for k in turns:
        blocks = lax.all_gather(blocks, axes[k])
    done = turns[::-1]
    back = [done.index(k) for k in range(len(axes))]
    blocks = blocks.transpose(*back, *range(len(axes), blocks.ndim))
    return blocks.reshape(-1, *value.shape)


def whole_of(value, axes, turns, dim):
    return joined_along(all_blocks(value, axes, turns), dim)


def in_one_piece(arrays, axis, dim, along):
    ends, at = ([], 0)
    for a in arrays[:-1]:
        at += a.shape[along]
        ends.append(at)
    both = jnp.concatenate(arrays, axis=along)
    return tuple(jnp.split(lax.all_gather(both, axis, axis=dim, tiled=True), ends, axis=along))


def from_behind(value, axis, steps):
    count = lax.axis_size(axis)
    pairs = [(source, (source + steps) % count) for source in range(count)]
    return lax.ppermute(value, axis, pairs)


def rms_norm(values, gain):
    values = values.astype(jnp.float32)
    scale = lax.rsqrt(jnp.mean(values * values, axis=-1, keepdims=True) + epsilon)
    return values * scale * gain.astype(jnp.float32)


def span_update(carry, block):
    state, prev_segment = carry
    inner_value, bin_value, cout_value, delta, log_decay, segment = block
    cumul = jnp.cumsum(log_decay, axis=0)
    order = jnp.arange(segment.shape[0])
    allowed = (order[:, None] >= order[None, :]) & (segment[:, None] == segment[None, :])
    differ = cumul[:, None, :] - cumul[None, :, :]
    factor = jnp.where(allowed[:, :, None], jnp.exp(jnp.minimum(differ, 0.0)), 0.0)
    intersection = jnp.dot(cout_value, bin_value.T, precision=highest)
    mixing = factor * intersection[:, :, None] * delta[None, :, :]
    within = jnp.einsum("tsh,shp->thp", mixing, inner_value, precision=highest)
    carried = jnp.where((segment == prev_segment)[:, None], jnp.exp(cumul), 0.0)
    across = jnp.einsum("tn,hpn->thp", cout_value, state, precision=highest) * carried[:, :, None]
    last_segment = segment[-1]
    keeping = (
        jnp.where((segment == last_segment)[:, None], jnp.exp(cumul[-1][None, :] - cumul), 0.0)
        * delta
    )
    fresh = jnp.einsum("sh,shp,sn->hpn", keeping, inner_value, bin_value, precision=highest)
    passing = jnp.where(prev_segment == last_segment, jnp.exp(cumul[-1]), 0.0)
    state = passing[:, None, None] * state + fresh
    return ((state, last_segment), within + across)


def combine_states(earlier, later):
    early_first, early_last, early_pass, early_state = earlier
    late_first, late_last, late_pass, late_state = later
    joined = (late_first == early_last) | (early_last < 0) | (late_first < 0)
    factor = jnp.where(joined, late_pass, 0.0)
    first = jnp.where(early_first < 0, late_first, early_first)
    last = jnp.where(late_last < 0, early_last, late_last)
    return (first, last, early_pass * factor, factor[:, None, None] * early_state + late_state)


def layer_pair(tokens, segment, weights):
    (
        norm_gain,
        w_mamba_in,
        w_ssm_param,
        ssm_rate,
        dt_bias,
        skip_gain,
        ssm_norm_gain,
        w_mamba_out,
        w_qkv,
        w_attn_out,
    ) = weights
    rows = tokens.shape[0]
    heads = ssm_rate.shape[0]
    offset = lax.axis_index(CTX) * rows
    normed = rms_norm(tokens, norm_gain[0]).astype(jnp.bfloat16)
    inner = jnp.dot(
        normed,
        lax.all_gather(w_mamba_in, CTX, axis=1, tiled=True),
        preferred_element_type=jnp.float32,
    ).astype(jnp.bfloat16)
    params = jnp.dot(normed, w_ssm_param, preferred_element_type=jnp.float32)
    bin_value = params[:, :STATE]
    cout_value = params[:, STATE : 2 * STATE]
    delta = jax.nn.softplus(params[:, 2 * STATE :] + dt_bias.astype(jnp.float32))
    log_decay = -delta * ssm_rate.astype(jnp.float32)
    inner_value = inner.astype(jnp.float32).reshape(rows, heads, HEAD_DIM)
    blocks = tuple(
        (
            item.reshape((rows // SPAN, SPAN) + item.shape[1:])
            for item in (inner_value, bin_value, cout_value, delta, log_decay, segment)
        )
    )
    start_carry = (jnp.zeros((heads, HEAD_DIM, STATE), jnp.float32), segment[0])
    (local_state, ignored), mixed = lax.scan(span_update, start_carry, blocks)
    device_decay = jnp.cumsum(log_decay, axis=0)
    through = jnp.where(segment[0] == segment[-1], jnp.exp(device_decay[-1]), 0.0)
    element = (segment[0], segment[-1], through, local_state)
    identity = (
        jnp.array(-1, jnp.int32),
        jnp.array(-1, jnp.int32),
        jnp.ones_like(through),
        jnp.zeros_like(local_state),
    )
    scanned = entering_2(element, CTX, combine_states, identity)
    incoming_segment = scanned[1]
    incoming_state = scanned[3]
    linked = jnp.where((segment == incoming_segment)[:, None], jnp.exp(device_decay), 0.0)
    entering = (
        jnp.einsum("tn,hpn->thp", cout_value, incoming_state, precision=highest)
        * linked[:, :, None]
    )
    mixed = (
        mixed.reshape(rows, heads, HEAD_DIM)
        + entering
        + skip_gain.astype(jnp.float32)[None, :, None] * inner_value
    )
    ssm_out = rms_norm(mixed.reshape(rows, INNER), ssm_norm_gain).astype(jnp.bfloat16)
    columns = ssm_out
    first = tokens.astype(jnp.float32) + jnp.dot(
        columns, whole_of(w_mamba_out, CTX, (1, 0, 2), 0), preferred_element_type=jnp.float32
    )
    hidden = rms_norm(first, norm_gain[1]).astype(jnp.bfloat16)
    projected = jnp.dot(
        hidden, lax.all_gather(w_qkv, CTX, axis=1, tiled=True), preferred_element_type=jnp.float32
    ).astype(jnp.bfloat16)
    groups = QUERY_HEADS // KV_HEADS
    query = projected[:, : QUERY_HEADS * ATTN_DIM].reshape(rows, KV_HEADS, groups, ATTN_DIM)
    keys = projected[:, QUERY_HEADS * ATTN_DIM : (QUERY_HEADS + KV_HEADS) * ATTN_DIM]
    values = projected[:, (QUERY_HEADS + KV_HEADS) * ATTN_DIM :]
    positions = offset + jnp.arange(rows)
    scale = 1.0 / math.sqrt(ATTN_DIM)
    top = jnp.full((KV_HEADS, groups, rows), -1e30, jnp.float32)
    key_piece, value_piece, segment_piece = (
        *in_one_piece((keys, values), CTX, 0, 1),
        lax.all_gather(segment, CTX, axis=0, tiled=True),
    )
    count = key_piece.shape[0]
    key_position = jnp.arange(count)
    scores = (
        jnp.einsum(
            "tkgd,skd->kgts",
            query,
            key_piece.reshape(count, KV_HEADS, ATTN_DIM),
            preferred_element_type=jnp.float32,
        )
        * scale
    )
    allowed = (key_position[None, :] <= positions[:, None]) & (
        segment_piece[None, :] == segment[:, None]
    )
    scores = jnp.where(allowed, scores, -1e30)
    new_top = jnp.maximum(top, jnp.max(scores, axis=-1))
    probs = jnp.where(allowed, jnp.exp(scores - new_top[..., None]), 0.0)
    total = jnp.sum(probs, axis=-1)
    attend_context = jnp.einsum(
        "kgts,skd->kgtd",
        probs.astype(jnp.bfloat16),
        value_piece.reshape(count, KV_HEADS, ATTN_DIM),
        preferred_element_type=jnp.float32,
    )
    top, total, context = (new_top, total, attend_context)
    context = context / total[..., None]
    context = (
        jnp.transpose(context, (2, 0, 1, 3))
        .reshape(rows, QUERY_HEADS * ATTN_DIM)
        .astype(jnp.bfloat16)
    )
    columns = context
    result = first + jnp.dot(
        columns,
        lax.all_gather(w_attn_out, CTX, axis=0, tiled=True),
        preferred_element_type=jnp.float32,
    )
    return result.astype(jnp.bfloat16)


def on_device(
    tokens,
    segment_ids,
    norm_gain,
    w_mamba_in,
    w_ssm_param,
    ssm_rate,
    dt_bias,
    skip_gain,
    ssm_norm_gain,
    w_mamba_out,
    w_qkv,
    w_attn_out,
):
    arrived = from_behind(
        (
            norm_gain,
            w_mamba_in,
            w_ssm_param,
            ssm_rate,
            dt_bias,
            skip_gain,
            ssm_norm_gain,
            w_mamba_out,
            w_qkv,
            w_attn_out,
        ),
        "blk",
        1,
    )
    section = tuple((item[0] for item in arrived))
    result = layer_pair(tokens[0], segment_ids[0], section)
    return result[None]


def solution(mesh):
    finer = Mesh(
        mesh.devices.reshape(mesh.shape["blk"], 8, 2, 2), ("blk", "ctx_0", "ctx_1", "ctx_2")
    )
    in_specs = (
        P("blk", CTX, None),
        P("blk", CTX),
        P("blk", None, None),
        P("blk", None, CTX),
        P("blk", None, None),
        P("blk", None),
        P("blk", None),
        P("blk", None),
        P("blk", None),
        P("blk", CTX, None),
        P("blk", None, CTX),
        P("blk", CTX, None),
    )
    out_specs = P("blk", CTX, None)
    return jax.shard_map(
        on_device, mesh=finer, in_specs=in_specs, out_specs=out_specs, check_vma=False
    )
```

profile of v0, /device:TPU:1, one launch (start us, length us, event | category | flops | bytes accessed | tf_op | source)
XLA Modules:
  0.0 555.8 jit_solution(135234453946944221)
XLA Ops:
  6.5 3.6 collective-permute-start.4
  10.1 5.0 collective-permute-done.4
  17.0 2.1 collective-permute-start.3
  21.0 2.3 collective-permute-start.1
  34.6 50.5 %all-gather.27.cloned.1.call-done = bf16[1,1024,2048]{1,2,0:T(8,128)(2,1)} async-done(((bf16[1,1024,64]{1,2,0:T(8,128)(2,1)}), bf16[1,1024,2048]{1,2,0:T(8,128)(2,1)}) %all-gather.27.cloned.1.call-update) | async-done | bytes 4194320 | tf_op jit(solution)/shard_map/all_gather | solution.py:171
  85.0 3.8 fusion.48
  88.8 2.2 reshape_reshape.4
  91.0 76.6 %while.15 = (s32[]{:T(128)}, f32[32,64,64]{2,1,0:T(8,128)S(1)}, s32[]{:T(128)}, f32[2,64,32,64]{1,0,3,2:T(2,128)}, s32[2,64]{1,0:T(2,128)}, /*index=5*/f32[2,64,...) while((s32[]{:T(128)}, f32[32,64,64]{2,1,0:T(8,128)S(1)}, ...), condition=%wide.region_3.4_spmd.clone, body=%wide.region_1.3_spmd.clone.sunk | while | flops 306858144 | bytes 9277010 | solution.py:187
  95.6 3.0 convolution_bitcast_fusion.2
  98.7 2.2 fusion.215
  103.2 25.4 %dynamic_update_slice.6 = f32[2,64,32,64]{1,0,3,2:T(2,128)} dynamic-update-slice(f32[2,64,32,64]{1,0,3,2:T(2,128)} %get-tuple-element.314, f32[1,64,32,64]{1,0,3,2:T(1,128)S(1)} %bitcast.295, s32[]{:T(128)S(6)} %copy.185, s32[]{:T(128)} %constant.29.clone.1..sunk, s32[]{:T(128)} %constant.29.clone.1..sunk, s32[]{:T(128)} %constant.29.clone.1..sunk) | dynamic-update-slice | bytes 1048580 | tf_op jit(solution)/shard_map/while/body/jit(dynamic_update_index_in_dim)/dynamic_update_slice | solution.py:187
  133.9 3.0 convolution_bitcast_fusion.2
  137.0 2.2 fusion.215
  141.5 25.4 %dynamic_update_slice.6 = f32[2,64,32,64]{1,0,3,2:T(2,128)} dynamic-update-slice(f32[2,64,32,64]{1,0,3,2:T(2,128)} %get-tuple-element.314, f32[1,64,32,64]{1,0,3,2:T(1,128)S(1)} %bitcast.295, s32[]{:T(128)S(6)} %copy.185, s32[]{:T(128)} %constant.29.clone.1..sunk, s32[]{:T(128)} %constant.29.clone.1..sunk, s32[]{:T(128)} %constant.29.clone.1..sunk) | dynamic-update-slice | bytes 1048580 | tf_op jit(solution)/shard_map/while/body/jit(dynamic_update_index_in_dim)/dynamic_update_slice | solution.py:187
  169.6 2.5 collective-permute-start.7
  172.1 6.2 %collective-permute-done.7 = bf16[1,64,1024]{2,1,0:T(8,128)(2,1)S(1)} collective-permute-done((bf16[1,64,1024]{2,1,0:T(8,128)(2,1)}, bf16[1,64,1024]{2,1,0:T(8,128)(2,1)S(1)}, u32[]{:S(2)}, u32[]{:S(2)}) %collective-permute-start.7) | collective-permute-done | bytes 131104 | tf_op jit(solution)/shard_map/ppermute | solution.py:109
  178.3 4.6 all_gather.79
  186.5 3.8 all-reduce.3
  197.4 26.2 %all-gather.29.cloned.1.call-done = bf16[16,64,1024]{2,1,0:T(8,128)(2,1)} async-done(((bf16[2,64,1024]{2,1,0:T(8,128)(2,1)}), bf16[16,64,1024]{2,1,0:T(8,128)(2,1)}) %all-gather.29.cloned.1.call-update) | async-done | bytes 2097168 | tf_op jit(solution)/shard_map/all_gather | solution.py:86
  228.4 3.1 all-reduce.4
  239.5 8.9 %all-reduce.5 = s32[16]{0:T(128)S(1)} all-reduce(s32[16]{0:T(128)S(1)} %fusion.174), channel_id=5, replica_groups=mesh['blk'=8,'ctx_0'=8,'ctx_1'=2,'ctx_2'=2] {'ctx_0'}, use_global_device_ids=true, to_apply=%add.5 | all-reduce | flops 16 | bytes 128
  264.1 3.0 collective-permute-start.8
  267.1 4.7 collective-permute-done.8
  273.2 2.1 collective-permute-start.5
  284.4 4.9 copy.121
  289.7 3.3 reshape.485
  299.8 37.0 %all-gather.41.cloned.1.call-done = f32[8,2049,64]{1,2,0:T(8,128)} async-done(((f32[1,2049,64]{1,2,0:T(8,128)}), f32[8,2049,64]{1,2,0:T(8,128)}) %all-gather.41.cloned.1.call-update) | async-done | bytes 4196368 | tf_op jit(solution)/shard_map/all_gather | solution.py:37
  336.7 3.7 fusion.183
  340.5 2.4 copy.142
  345.5 2.5 copy.139
  347.9 2.4 copy.138
  350.3 2.4 copy.137
  352.7 2.4 copy.136
  356.6 6.6 %multiply_reduce_fusion = (f32[128]{0:T(128)S(1)}, f32[128,32,64]{0,2,1:T(8,128)S(1)}) fusion(f32[32]{0:T(128)S(1)} %bitcast_convert_fusion, f32[128,2048]{0,1:T(8,128)S(1)} %copy.120, f32[128,32,64]{0,2,1:T(8,128)S(1)} %copy-done.5, f32[128,32]{0,1:T(8,128)S(1)} %exponential_select_fusion.2, f32[32,64,64]{2,1,0:T(8,128)} %bitcast.297, ...), kind=kOutput, calls=%fused_computation.76 | convolution fusion | flops 207748992 | bytes 15780236 | tf_op jit(solution)/shard_map/tn,hpn->thp/dot_general | solution.py:202
  364.5 39.8 %all-gather.33.cloned.1.call-done = bf16[1,1024,2048]{1,2,0:T(8,128)(2,1)} async-done(((bf16[1,1024,64]{1,2,0:T(8,128)(2,1)}), bf16[1,1024,2048]{1,2,0:T(8,128)(2,1)}) %all-gather.33.cloned.1.call-update) | async-done | bytes 4194320 | tf_op jit(solution)/shard_map/all_gather | solution.py:217
  404.3 3.7 fusion.51
  408.8 2.5 collective-permute-start.9
  411.3 32.6 %all-gather.9 = s32[1,4096]{1,0:T(1,128)S(1)} all-gather(s32[1,128]{1,0:T(1,128)S(1)} %copy-done.12), channel_id=11, replica_groups=mesh['blk'=8,'ctx_0'=8,'ctx_1'=2,'ctx_2'=2] {'ctx_0','ctx_1','ctx_2'}, dimensions={1}, use_global_device_ids=true | all-gather | bytes 16896 | tf_op jit(solution)/shard_map/all_gather | solution.py:228
  446.6 34.0 %all-gather.25.cloned.1.call-done = bf16[4096,1024]{1,0:T(8,128)(2,1)} async-done(((bf16[128,1024]{1,0:T(8,128)(2,1)}), bf16[4096,1024]{1,0:T(8,128)(2,1)}) %all-gather.25.cloned.1.call-update) | async-done | bytes 8388624 | tf_op jit(solution)/shard_map/all_gather | solution.py:103
  480.6 5.8 %fusion.182 = (bf16[4096,512]{1,0:T(8,128)(2,1)}, bf16[4096,512]{1,0:T(8,128)(2,1)}) fusion(bf16[4096,1024]{1,0:T(8,128)(2,1)} %all-gather.25.cloned.1.call-done), kind=kLoop, calls=%fused_computation.239 | loop fusion | bytes 16777216 | tf_op jit(solution)/shard_map/split | solution.py:103
  486.4 7.0 %reshape.498 = bf16[4096,4,128]{2,1,0:T(4,128)(2,1)} reshape(bf16[4096,512]{1,0:T(8,128)(2,1)} %get-tuple-element.166) | data formatting | bytes 8388608 | tf_op jit(solution)/shard_map/reshape | solution.py:236
  493.3 9.8 %fusion.33 = (f32[4,2,128]{2,1,0:T(2,128)S(1)}, f32[4,4096,128,2]{2,1,3,0:T(8,128)}) fusion(pred[128,4096]{0,1:T(8,128)(4,1)S(1)} %fusion.56, bf16[128,4,2,128]{3,2,1,0:T(2,128)(2,1)S(1)} %reshape.499, bf16[4096,4,128,1]{2,1,0,3:T(4,128)(2,1)} %bitcast.311), kind=kOutput, calls=%fused_computation.50 | convolution fusion | flops 1086323712 | bytes 21762048 | tf_op jit(solution)/shard_map/tkgd,skd->kgts/dot_general | solution.py:233
  503.1 6.5 %copy.149 = bf16[4096,512]{0,1:T(8,128)(2,1)} copy(bf16[4096,512]{1,0:T(8,128)(2,1)} %get-tuple-element.167) | data formatting | bytes 8388608 | tf_op jit(solution)/shard_map/reshape | solution.py:251
  509.6 8.3 %fusion.34 = f32[4,2,128]{2,1,0:T(2,128)S(1)} fusion(f32[4,4096,128,2]{2,1,3,0:T(8,128)} %get-tuple-element.226, f32[4,2,128]{2,1,0:T(2,128)S(1)} %broadcast_maximum_fusion, pred[128,4096]{0,1:T(8,128)(4,1)S(1)} %fusion.56), kind=kLoop, calls=%fused_computation.51 | loop fusion | flops 20970496 | bytes 17309696 | tf_op jit(solution)/shard_map/reduce_sum | solution.py:247
  517.8 2.5 copy-done
  520.4 6.5 %fusion.110 = bf16[128,4,2,128]{0,3,2,1:T(8,128)(2,1)S(1)} fusion(bf16[4096,4,128,1]{0,2,3,1:T(8,128)(2,1)} %bitcast.310, f32[4,4096,128,2]{2,1,3,0:T(8,128)S(1)} %copy-done, f32[4,2,128]{2,1,0:T(2,128)S(1)} %broadcast_maximum_fusion, pred[128,4096]{0,1:T(8,128)(4,1)S(1)} %fusion.56, f32[128,4,2]{0,2,1:T(2,128)S(1)} %bitcast.326), kind=kOutput, calls=%fused_computation.116 | convolution fusion | flops 1094975488 | bytes 21766144 | tf_op jit(solution)/shard_map/kgts,skd->kgtd/dot_general | solution.py:248
  526.8 19.3 %all-gather.35.cloned.1.call-done = bf16[1,1024,1024]{2,1,0:T(8,128)(2,1)} async-done(((bf16[1,32,1024]{2,1,0:T(8,128)(2,1)}), bf16[1,1024,1024]{2,1,0:T(8,128)(2,1)}) %all-gather.35.cloned.1.call-update) | async-done | bytes 2097168 | tf_op jit(solution)/shard_map/all_gather | solution.py:264
  546.1 2.8 fusion.67
  (191 shorter events, 58.9 us)
Async XLA Ops:
  6.5 78.5 %all-gather.27.cloned.1.call-start = ((), (), s32[]{:S(2)}) async-start(), calls=%async_computation.1 | async-start | bytes 4325376 | tf_op jit(solution)/shard_map/all_gather | solution.py:171
  6.5 8.6 %collective-permute-start.4 = (bf16[1,1024,64]{1,2,0:T(8,128)(2,1)}, bf16[1,1024,64]{1,2,0:T(8,128)(2,1)S(1)}, u32[]{:S(2)}, u32[]{:S(2)}) collective-permute-start(bf16[1,1024,64]{1,2,0:T(8,128)(2,1)} %param.17), channel_id=1, source_target_pairs={{0,32},{32,64},{64,96},{96,128},{128,160},{160,192},{192,224},{224... | collective-permute-start | bytes 393224 | tf_op jit(solution)/shard_map/ppermute | solution.py:109
  15.1 0.7 copy-start.9
  15.8 177.9 %all-gather.37.cloned.1.call-start = ((), (), s32[]{:S(2)}) async-start(), calls=%async_computation.6 | async-start | bytes 1671168 | tf_op jit(solution)/shard_map/all_gather | solution.py:37
  15.8 14.4 %collective-permute-start = (bf16[1,2,1024]{2,1,0:T(2,128)(2,1)}, bf16[1,2,1024]{2,1,0:T(2,128)(2,1)S(1)}, u32[]{:S(2)}, u32[]{:S(2)}) collective-permute-start(bf16[1,2,1024]{2,1,0:T(2,128)(2,1)} %param.16), channel_id=1, source_target_pairs={{0,32},{32,64},{64,96},{96,128},{128,160},{160,192},{192,224},{224... | collective-permute-start | bytes 12296 | tf_op jit(solution)/shard_map/ppermute | solution.py:109
  17.0 13.2 %collective-permute-start.3 = (bf16[1,32]{1,0:T(2,128)(2,1)}, bf16[1,32]{1,0:T(2,128)(2,1)S(1)}, u32[]{:S(2)}, u32[]{:S(2)}) collective-permute-start(bf16[1,32]{1,0:T(2,128)(2,1)} %param.19), channel_id=1, source_target_pairs={{0,32},{32,64},{64,96},{96,128},{128,160},{160,192},{192,224},{224... | collective-permute-start | bytes 200 | tf_op jit(solution)/shard_map/ppermute | solution.py:109
  19.1 11.0 %collective-permute-start.2 = (bf16[1,32]{1,0:T(2,128)(2,1)}, bf16[1,32]{1,0:T(2,128)(2,1)S(1)}, u32[]{:S(2)}, u32[]{:S(2)}) collective-permute-start(bf16[1,32]{1,0:T(2,128)(2,1)} %param.20), channel_id=1, source_target_pairs={{0,32},{32,64},{64,96},{96,128},{128,160},{160,192},{192,224},{224... | collective-permute-start | bytes 200 | tf_op jit(solution)/shard_map/ppermute | solution.py:109
  21.0 10.9 %collective-permute-start.1 = (bf16[1,1024,160]{1,2,0:T(8,128)(2,1)}, bf16[1,1024,160]{1,2,0:T(8,128)(2,1)S(1)}, u32[]{:S(2)}, u32[]{:S(2)}) collective-permute-start(bf16[1,1024,160]{1,2,0:T(8,128)(2,1)} %param.18), channel_id=1, source_target_pairs={{0,32},{32,64},{64,96},{96,128},{128,160},{160,192},{192,224},{224... | collective-permute-start | bytes 983048 | tf_op jit(solution)/shard_map/ppermute | solution.py:109
  33.2 1.4 copy-start.7
  88.8 2.2 copy-start.2
  167.9 56.9 %copy-start.18 = (u32[256]{0:T(256)S(1)}, u32[256]{0:T(256)}, u32[]{:S(2)}) copy-start(u32[256]{0:T(256)} %constant.109) | copy-start | bytes 3076
  167.9 67.0 %copy-start.17 = (u32[256]{0:T(256)S(1)}, u32[256]{0:T(256)}, u32[]{:S(2)}) copy-start(u32[256]{0:T(256)} %constant.114) | copy-start | bytes 3076
  169.6 53.9 %all-gather.29.cloned.1.call-start = ((), (), s32[]{:S(2)}) async-start(), calls=%async_computation.2 | async-start | bytes 2359296 | tf_op jit(solution)/shard_map/all_gather | solution.py:86
  169.6 8.7 %collective-permute-start.7 = (bf16[1,64,1024]{2,1,0:T(8,128)(2,1)}, bf16[1,64,1024]{2,1,0:T(8,128)(2,1)S(1)}, u32[]{:S(2)}, u32[]{:S(2)}) collective-permute-start(bf16[1,64,1024]{2,1,0:T(8,128)(2,1)} %param.23), channel_id=1, source_target_pairs={{0,32},{32,64},{64,96},{96,128},{128,160},{160,192},{192,224},{224... | collective-permute-start | bytes 393224 | tf_op jit(solution)/shard_map/ppermute | solution.py:109
  182.9 77.6 %all-gather.39.cloned.1.call-start = ((), (), s32[]{:S(2)}) async-start(), calls=%async_computation.7 | async-start | bytes 1671168 | tf_op jit(solution)/shard_map/all_gather | solution.py:37
  195.1 69.0 %copy-start.13 = (bf16[1,1024,64]{1,2,0:T(8,128)(2,1)S(1)}, bf16[1,1024,64]{1,2,0:T(8,128)(2,1)}, u32[]{:S(2)}) copy-start(bf16[1,1024,64]{1,2,0:T(8,128)(2,1)} %param.24) | copy-start | bytes 393220
  196.4 76.2 %copy-start.15 = (bf16[1,2048]{1,0:T(2,128)(2,1)S(1)}, bf16[1,2048]{1,0:T(2,128)(2,1)}, u32[]{:S(2)}) copy-start(bf16[1,2048]{1,0:T(2,128)(2,1)} %param.22) | copy-start | bytes 12292
  196.4 76.9 %copy-start.16 = (bf16[1,32]{1,0:T(2,128)(2,1)S(1)}, bf16[1,32]{1,0:T(2,128)(2,1)}, u32[]{:S(2)}) copy-start(bf16[1,32]{1,0:T(2,128)(2,1)} %param.21) | copy-start | bytes 196
  196.4 87.7 %copy-start.12 = (s32[1,128]{1,0:T(1,128)S(1)}, s32[1,128]{1,0:T(1,128)}, u32[]{:S(2)}) copy-start(s32[1,128]{1,0:T(1,128)} %param.15) | copy-start | bytes 1540
  197.3 87.1 %all-gather.31.cloned.1.call-start = ((), (), s32[]{:S(2)}) async-start(), calls=%async_computation.3 | async-start | bytes 6291456 | tf_op jit(solution)/shard_map/all_gather | solution.py:86
  223.6 113.2 %all-gather.41.cloned.1.call-start = ((), (), s32[]{:S(2)}) async-start(), calls=%async_computation.8 | async-start | bytes 5013504 | tf_op jit(solution)/shard_map/all_gather | solution.py:37
  264.1 140.2 %all-gather.33.cloned.1.call-start = ((), (), s32[]{:S(2)}) async-start(), calls=%async_computation.4 | async-start | bytes 4325376 | tf_op jit(solution)/shard_map/all_gather | solution.py:217
  264.1 7.7 %collective-permute-start.8 = (bf16[1,1024,64]{1,2,0:T(8,128)(2,1)S(1)}, bf16[1,1024,64]{1,2,0:T(8,128)(2,1)S(1)}, u32[]{:S(2)}, u32[]{:S(2)}) collective-permute-start(bf16[1,1024,64]{1,2,0:T(8,128)(2,1)S(1)} %copy-done.13), channel_id=1, source_target_pairs={{0,32},{32,64},{64,96},{96,128},{128,160},{160,192},{192,224},{224... | collective-permute-start | bytes 393224 | tf_op jit(solution)/shard_map/ppermute | solution.py:109
  271.8 0.7 copy-start.8
  272.5 208.1 %all-gather.25.cloned.1.call-start = ((), (), s32[]{:S(2)}) async-start(), calls=%async_computation | async-start | bytes 8650752 | tf_op jit(solution)/shard_map/all_gather | solution.py:103
  272.6 11.6 %collective-permute-start.6 = (bf16[1,2048]{1,0:T(2,128)(2,1)S(1)}, bf16[1,2048]{1,0:T(2,128)(2,1)S(1)}, u32[]{:S(2)}, u32[]{:S(2)}) collective-permute-start(bf16[1,2048]{1,0:T(2,128)(2,1)S(1)} %copy-done.15), channel_id=1, source_target_pairs={{0,32},{32,64},{64,96},{96,128},{128,160},{160,192},{192,224},{224... | collective-permute-start | bytes 12296 | tf_op jit(solution)/shard_map/ppermute | solution.py:109
  273.2 10.9 %collective-permute-start.5 = (bf16[1,32]{1,0:T(2,128)(2,1)S(1)}, bf16[1,32]{1,0:T(2,128)(2,1)S(1)}, u32[]{:S(2)}, u32[]{:S(2)}) collective-permute-start(bf16[1,32]{1,0:T(2,128)(2,1)S(1)} %copy-done.16), channel_id=1, source_target_pairs={{0,32},{32,64},{64,96},{96,128},{128,160},{160,192},{192,224},{224... | collective-permute-start | bytes 200 | tf_op jit(solution)/shard_map/ppermute | solution.py:109
  284.4 4.9 copy-start.3
  289.3 3.7 copy-start.4
  345.5 11.0 %slice-start = ((f32[8,2049,64]{1,2,0:T(8,128)}), f32[8,1,64]{1,2,0:T(8,128)S(1)}, s32[]{:S(2)}) async-start(f32[8,2049,64]{1,2,0:T(8,128)} %all-gather.41.cloned.1.call-done), calls=%async_computation.9 | async-start | bytes 524288 | tf_op jit(solution)/shard_map/slice | solution.py:39
  345.5 11.1 %copy-start.5 = (f32[128,32,64]{0,2,1:T(8,128)S(1)}, f32[128,32,64]{0,2,1:T(8,128)}, u32[]{:S(2)}) copy-start(f32[128,32,64]{0,2,1:T(8,128)} %reshape.485) | copy-start | bytes 3145732
  356.6 7.1 %copy-start.1 = (bf16[8,2,2,64,1024]{4,3,2,1,0:T(8,128)(2,1)S(1)}, bf16[8,2,2,64,1024]{4,3,2,1,0:T(8,128)(2,1)}, u32[]{:S(2)}) copy-start(bf16[8,2,2,64,1024]{4,3,2,1,0:T(8,128)(2,1)} %copy.121) | copy-start | bytes 12582916
  356.6 7.1 %copy-start.6 = (bf16[1,128,1024]{2,1,0:T(8,128)(2,1)S(1)}, bf16[1,128,1024]{2,1,0:T(8,128)(2,1)}, u32[]{:S(2)}) copy-start(bf16[1,128,1024]{2,1,0:T(8,128)(2,1)} %param.14) | copy-start | bytes 786436
  363.2 41.1 %copy-start.11 = (f32[1,1,1024]{2,1,0:T(1,128)S(1)}, f32[1,1,1024]{2,1,0:T(1,128)}, u32[]{:S(2)}) copy-start(f32[1,1,1024]{2,1,0:T(1,128)} %get-tuple-element.184) | copy-start | bytes 12292
  364.5 44.3 %copy-start.14 = (bf16[1,32,1024]{2,1,0:T(8,128)(2,1)S(1)}, bf16[1,32,1024]{2,1,0:T(8,128)(2,1)}, u32[]{:S(2)}) copy-start(bf16[1,32,1024]{2,1,0:T(8,128)(2,1)} %param.25) | copy-start | bytes 196612
  408.8 137.3 %all-gather.35.cloned.1.call-start = ((), (), s32[]{:S(2)}) async-start(), calls=%async_computation.5 | async-start | bytes 2162688 | tf_op jit(solution)/shard_map/all_gather | solution.py:264
  408.8 36.9 %collective-permute-start.9 = (bf16[1,32,1024]{2,1,0:T(8,128)(2,1)S(1)}, bf16[1,32,1024]{2,1,0:T(8,128)(2,1)S(1)}, u32[]{:S(2)}, u32[]{:S(2)}) collective-permute-start(bf16[1,32,1024]{2,1,0:T(8,128)(2,1)S(1)} %copy-done.14), channel_id=1, source_target_pairs={{0,32},{32,64},{64,96},{96,128},{128,160},{160,192},{192,224},{224... | collective-permute-start | bytes 196616 | tf_op jit(solution)/shard_map/ppermute | solution.py:109
  445.8 0.6 copy-start.10
  509.6 10.8 %copy-start = (f32[4,4096,128,2]{2,1,3,0:T(8,128)S(1)}, f32[4,4096,128,2]{2,1,3,0:T(8,128)}, u32[]{:S(2)}) copy-start(f32[4,4096,128,2]{2,1,3,0:T(8,128)} %get-tuple-element.226) | copy-start | bytes 50331652
Sparse Core Ops, SparseCore 0:
  15.9 69.0 all-gather.26
  169.7 14.7 all-gather.36
  186.3 37.2 all-gather.28
  225.2 29.6 all-gather.38
  256.5 20.8 all-gather.30
  279.1 57.6 all-gather.40
  338.6 65.6 all-gather.32
  408.9 71.6 all-gather.24
  482.4 63.6 all-gather.34
where the time goes:
time: 564 us; the launch traced here: 556 us
  waiting for transfers between devices  224 us (40%)
  local copies, waits for them, and re-layouts  130 us (23%)
  blocking collectives  53 us (9%)
  between operations  49.9 us (9%)
  matrix products  49.1 us (9%)
  other arithmetic  24.8 us (4%)
  starting transfers between devices  22 us (4%)
    dynamic_update_slice x2, local copies, waits for them, and re-layouts, layer_pair(): (local_state, ignored), mixed = lax.scan(span_update, start_carry, blocks)  50.9 us
    all_gather x1, waiting for transfers between devices, layer_pair(): lax.all_gather(w_mamba_in, CTX, axis=1, tiled=True)  50.5 us
    all_gather x1, waiting for transfers between devices, layer_pair(): lax.all_gather(w_qkv, CTX, axis=1, tiled=True)  39.8 us
    all_gather x3, waiting for transfers between devices, gathered_once(): both, at, found = (lax.all_gather(jnp.concatenate(lines), axis), 0, {})  37 us
    all_gather x1, waiting for transfers between devices, in_one_piece(): lax.all_gather(both, axis, axis=dim, tiled=True)  34 us
    all_gather x1, blocking collectives, layer_pair(): lax.all_gather(segment, CTX, axis=0, tiled=True)  32.6 us
    all_gather x2, waiting for transfers between devices, all_blocks(): blocks = lax.all_gather(blocks, axes[k])  26.2 us
    ppermute x10, starting transfers between devices, from_behind(): return lax.ppermute(value, axis, pairs)  21.7 us
  transfers between devices with their start and end apart: 19, of which 10 were waited for; matrix products, arithmetic and copies ran while one was open for 20% of the time, Pallas kernels for 0%

commit v1 on v0

v1 whole, which is shorter than its diff:
```python
import math

import jax
import jax.numpy as jnp
from jax import lax
from jax.experimental import pallas as pl
from jax.experimental.pallas import tpu as pltpu
from jax.sharding import Mesh
from jax.sharding import PartitionSpec as P


MODEL = 1024
INNER = 2048
HEAD_DIM = 64
STATE = 64
ATTN_DIM = 128
HEADS = 8
ROWS = 128
TOKENS = 512
PLANES = 8
LANES = 128
CTX = ("z", "x", "c")
epsilon = 1e-05
highest = lax.Precision.HIGHEST
f32 = jnp.float32
bf16 = jnp.bfloat16


def moved(value, axis, target):
    count = lax.axis_size(axis)
    return lax.ppermute(value, axis, [(i, target(i)) for i in range(count)])


def swapped(value, axis):
    return moved(value, axis, lambda i: 1 - i)


def ring(value, cut, after=(None, None, None)):
    found = {0: [value]}
    up = down = value
    half = PLANES // 2
    for k in range(1, half + 1):
        if k > 1 and after[k - 2] is not None:
            up, down, _ = lax.optimization_barrier((up, down, after[k - 2]))
            found[PLANES - k + 1], found[k - 1] = [up], [down]
        if k == half and cut is not None:
            up, down = up[:cut], down[cut:]
        up = moved(up, "z", lambda i: (i + 1) % PLANES)
        if k == half and cut is None:
            found[half] = [up]
            break
        down = moved(down, "z", lambda i: (i - 1) % PLANES)
        if k < half:
            found[PLANES - k], found[k] = [up], [down]
        else:
            found[half] = [up, down]
    return [part for k in range(PLANES) for part in found[k]]


smem = pl.BlockSpec(memory_space=pltpu.SMEM)
vmem = pl.BlockSpec(memory_space=pltpu.VMEM)
whole = pl.BlockSpec(memory_space=pl.ANY)


def local(kernel, outs, in_specs, scratch, flops, size, *operands, aliases=None):
    return pl.pallas_call(
        kernel,
        out_shape=tuple(jax.ShapeDtypeStruct(shape, kind) for shape, kind in outs),
        in_specs=in_specs,
        out_specs=tuple(smem if len(shape) == 1 else vmem for shape, _ in outs),
        input_output_aliases=aliases or {},
        scratch_shapes=scratch,
        cost_estimate=pl.CostEstimate(flops=flops, bytes_accessed=size, transcendentals=0),
    )(*operands)


def fetch(views, target, sems, first=0):
    copies = []
    for n, (k, view, offset, rows) in enumerate(views):
        copy = pltpu.make_async_copy(view, target(k, offset, rows), sems.at[first + n])
        copy.start()
        copies.append(copy)
    return copies


def views(refs, low, high, cut=None):
    if cut is None:
        return [(k, ref.at[low:high], 0, high - low) for k, ref in enumerate(refs)]
    found = []
    for k in range(PLANES):
        if k != PLANES // 2:
            found.append((k, refs[k + (k > PLANES // 2)].at[low:high], 0, high - low))
            continue
        if low < cut:
            end = min(high, cut)
            found.append((k, refs[k].at[low:end], 0, end - low))
        if high > cut:
            begin = max(low, cut)
            found.append((k, refs[k + 1].at[begin - cut:high - cut], begin - low, high - begin))
    return found


def placed(at_ref, scr, size):
    return lambda k, offset, rows: scr.at[
        pl.ds(pl.multiple_of(plane_of(at_ref, k) * size + offset, 16), rows)]


def plane_of(at_ref, k):
    return lax.rem(at_ref[0] + k, PLANES)


def quad_places(at_ref):
    x, c = at_ref[1], at_ref[2]
    return [2 * x + c, 2 * (1 - x) + c, 2 * x + 1 - c, 2 * (1 - x) + 1 - c]


def rows_at(block, size):
    return pl.ds(pl.multiple_of(block * size, size), size)


def split(value, parts):
    found = []
    for _ in range(parts):
        piece = value.astype(bf16)
        found.append(piece)
        value = value - piece.astype(f32)
    return found


def rms(values, gain):
    scale = lax.rsqrt(jnp.mean(values * values, axis=-1, keepdims=True) + epsilon)
    return values * scale * gain


def lane_masks():
    row = lax.broadcasted_iota(jnp.int32, (LANES, LANES), 0)
    col = lax.broadcasted_iota(jnp.int32, (LANES, LANES), 1)
    return row >= col, col < HEAD_DIM, col


def steps(raw, head_ref):
    raw = raw + head_ref[0:1, :]
    delta = jnp.maximum(raw, 0.0) + jnp.log1p(jnp.exp(-jnp.abs(raw)))
    return delta, -delta * head_ref[1:2, :]


def enter_kernel(at_ref, *refs):
    blocks, shards = refs[:4], refs[4:12]
    wout_ref, gain_ref, wprm_ref, head_ref = refs[12:16]
    u_ref, prm_ref, segc_ref, segr_ref, pack_ref = refs[16:21]
    x_scr, w_scr, n_scr, sems = refs[21:]
    places = quad_places(at_ref)
    copies = fetch([(i, blocks[i], 0, 0) for i in range(4)], lambda i, *_: x_scr.at[places[i]], sems)
    copies_w = fetch(views(shards, 0, 64), placed(at_ref, w_scr, 64), sems, 4)
    for copy in copies:
        copy.wait()
    tri, left, col = lane_masks()
    trif = tri.astype(f32)

    def normed(b, _):
        at = rows_at(b, ROWS)
        n_scr[at, :] = rms(x_scr[b, 0:ROWS, :].astype(f32), gain_ref[...].astype(f32)).astype(bf16)
        seg = x_scr[b, ROWS:ROWS + 16, 0:LANES].astype(f32)[0:1, :]
        segr_ref[:, at] = seg
        segc_ref[at, :] = jnp.transpose(jnp.broadcast_to(seg, (LANES, LANES)))
        return 0

    lax.fori_loop(0, 4, normed, 0)
    prm_ref[...] = jnp.dot(n_scr[...], wprm_ref[...], preferred_element_type=f32)
    cums, deltas = [], []
    offset = jnp.zeros((1, LANES), f32)
    for i in range(4):
        at = pl.ds(i * LANES, LANES)
        delta, log_decay = steps(prm_ref[at, LANES:2 * LANES], head_ref)
        cum = jnp.dot(trif, log_decay, precision=highest, preferred_element_type=f32) + offset
        offset = cum[LANES - 1:, :]
        cums.append(cum)
        deltas.append(delta)
    bin_t = jnp.concatenate(
        [jnp.transpose(prm_ref[pl.ds(i * LANES, LANES), 0:LANES])[STATE:, :] for i in range(4)],
        axis=1).astype(bf16)
    seg_last = segr_ref[:, TOKENS - 1:]
    for copy in copies_w:
        copy.wait()
    u_ref[...] = lax.dot_general(
        n_scr[...], w_scr[...], (((1,), (1,)), ((), ())), preferred_element_type=f32).astype(bf16)
    keeps = []
    for i in range(4):
        segc = segc_ref[pl.ds(i * LANES, LANES), :]
        keeps.append(jnp.where(segc == seg_last, jnp.exp(offset - cums[i]), 0.0) * deltas[i])
    for p in range(HEADS // 2):
        lanes = pl.ds(p * LANES, LANES)
        kept = []
        for i in range(4):
            up = u_ref[pl.ds(i * LANES, LANES), lanes].astype(f32)
            kept.append(up * jnp.where(left, keeps[i][:, 2 * p:2 * p + 1], keeps[i][:, 2 * p + 1:2 * p + 2]))
        kept = jnp.concatenate(kept, axis=0).astype(bf16)
        state = jnp.dot(bin_t, kept, preferred_element_type=f32).astype(bf16)
        pack_ref[0:32, lanes] = state[0:32]
        pack_ref[0:32, pl.ds(512 + p * LANES, LANES)] = state[32:64]
    facts = jnp.where(col[:1] < HEADS, offset, 0.0)
    facts = jnp.where(col[:1] == HEADS, seg_last, facts)
    segr = segr_ref[...]
    for v in range(4):
        count = jnp.sum(jnp.where(segr == float(v), 1.0, 0.0), axis=1, keepdims=True)
        facts = jnp.where(col[:1] == HEADS + 1 + v, count, facts)
    pieces = [piece.astype(f32) for piece in split(facts, 3)]
    rows16 = lax.broadcasted_iota(jnp.int32, (16, LANES), 0)
    fact_rows = jnp.where(rows16 == 0, pieces[0], jnp.where(rows16 == 1, pieces[1], jnp.where(rows16 == 2, pieces[2], 0.0)))
    pack_ref[32:48, :] = jnp.zeros((16, MODEL), bf16)
    pack_ref[32:48, 0:LANES] = fact_rows.astype(bf16)
    pack_ref[48:112, :] = wout_ref[...]


def space_kernel(u_ref, prm_ref, head_ref, skip_ref, segc_ref, segr_ref, y_ref, cum_ref, st_ref):
    tri, left, _ = lane_masks()
    trif = tri.astype(f32)
    st_ref[...] = jnp.zeros_like(st_ref)

    def chunk(i, carry):
        offset, seg_prev = carry
        at = rows_at(i, LANES)
        delta, log_decay = steps(prm_ref[at, LANES:2 * LANES], head_ref)
        cum = jnp.dot(trif, log_decay, precision=highest, preferred_element_type=f32)
        cum_ref[at, :] = cum + offset
        last = cum[LANES - 1:, :]
        cum_t = jnp.transpose(cum)
        delta_t = jnp.transpose(delta)
        both = prm_ref[at, 0:LANES]
        cout = both[:, :STATE].astype(bf16)
        bin_t = jnp.transpose(both)[STATE:, :].astype(bf16)
        cross = jnp.dot(cout, bin_t, preferred_element_type=f32)
        segc = segc_ref[at, :]
        segr = segr_ref[:, at]
        seg_last = segc[LANES - 1:, :]
        carried = jnp.where(segc == seg_prev, jnp.exp(cum), 0.0)
        keep = jnp.where(segc == seg_last, jnp.exp(last - cum), 0.0) * delta
        passing = jnp.where(seg_prev == seg_last, jnp.exp(last), 0.0)
        crossed = jnp.where(tri & (segc == segr), cross, 0.0)
        for p in range(HEADS // 2):
            a, b = 2 * p, 2 * p + 1
            lanes = pl.ds(p * LANES, LANES)
            up = u_ref[at, lanes]
            mix = []
            for h in (a, b):
                differ = cum[:, h:h + 1] - cum_t[h:h + 1, :]
                mix.append(jnp.exp(jnp.minimum(differ, 0.0)) * crossed * delta_t[h:h + 1, :])
            mix = jnp.concatenate(mix, axis=1).astype(bf16)
            zero = jnp.zeros_like(up)
            halves = jnp.concatenate([jnp.where(left, up, zero), jnp.where(left, zero, up)], axis=0)
            y = jnp.dot(mix, halves, preferred_element_type=f32)
            state = st_ref[:, lanes]
            y = y + jnp.dot(cout, state.astype(bf16), preferred_element_type=f32) * jnp.where(
                left, carried[:, a:a + 1], carried[:, b:b + 1])
            uf = up.astype(f32)
            y_ref[at, lanes] = y + skip_ref[:, lanes] * uf
            kept = (uf * jnp.where(left, keep[:, a:a + 1], keep[:, b:b + 1])).astype(bf16)
            pass_lane = jnp.where(left[:1], passing[:, a:a + 1], passing[:, b:b + 1])
            st_ref[:, lanes] = pass_lane * state + jnp.dot(bin_t, kept, preferred_element_type=f32)
        return offset + last, seg_last

    lax.fori_loop(0, TOKENS // LANES, chunk, (jnp.zeros((1, LANES), f32), segc_ref[0:1, :]))


def leave_kernel(at_ref, *refs):
    packs = refs[0:9]
    y_ref, cum_ref, prm_ref, segc_ref, gain_ref = refs[9:14]
    keep_ref, send_ref, start_ref, first_ref = refs[14:18]
    p_scr, w_scr, m_scr, s_scr, sems = refs[18:]
    copies = fetch(views(packs, 0, 48, 48), lambda k, *_: p_scr.at[k], sems)
    copies_w = fetch(views(packs, 48, 112, 48), placed(at_ref, w_scr, 64), sems, PLANES)
    z, x, c = at_ref[0], at_ref[1], at_ref[2]
    segc = segc_ref[...]
    seg_first = segc[0:1, 0:1]
    left = lax.broadcasted_iota(jnp.int32, (TOKENS, LANES), 1) < HEAD_DIM
    entering = jnp.where(segc == seg_first, jnp.exp(cum_ref[...]), 0.0)
    cout = prm_ref[:, 0:STATE].astype(bf16)
    for copy in copies:
        copy.wait()
    acc = jnp.zeros((1, LANES), f32)
    totals = jnp.zeros((1, LANES), f32)
    decays = [None] * PLANES
    for k in range(PLANES - 1, -1, -1):
        facts = p_scr[k, 32:48, 0:LANES].astype(f32)
        facts = facts[0:1] + facts[1:2] + facts[2:3]
        totals = totals + facts
        if k > 0:
            valid = jnp.where(z + k >= PLANES, 1.0, 0.0)
            decays[k] = jnp.where(facts[:, HEADS:HEADS + 1] == seg_first, jnp.exp(acc), 0.0) * valid
            acc = acc + facts
    below = jnp.zeros((TOKENS, LANES), f32)
    for v in range(4):
        below = below + jnp.where(segc > float(v), totals[:, HEADS + 1 + v:HEADS + 2 + v], 0.0)
    start_ref[...] = below.astype(jnp.int32)
    first_ref[0] = jnp.min(below[0:8, :]).astype(jnp.int32) // TOKENS
    squares = jnp.zeros((TOKENS, 1), f32)
    for p in range(HEADS // 2):
        lanes = pl.ds(p * LANES, LANES)
        low = jnp.zeros((32, LANES), f32)
        high = jnp.zeros((32, LANES), f32)
        for k in range(1, PLANES):
            decay = jnp.where(left[:1], decays[k][:, 2 * p:2 * p + 1], decays[k][:, 2 * p + 1:2 * p + 2])
            low = low + p_scr[k, 0:32, lanes].astype(f32) * decay
            high = high + p_scr[k, 0:32, pl.ds(512 + p * LANES, LANES)].astype(f32) * decay
        state = jnp.concatenate([low, high], axis=0).astype(bf16)
        factor = jnp.where(left, entering[:, 2 * p:2 * p + 1], entering[:, 2 * p + 1:2 * p + 2])
        mixed = y_ref[:, lanes] + jnp.dot(cout, state, preferred_element_type=f32) * factor
        squares = squares + jnp.sum(mixed * mixed, axis=1, keepdims=True)
        m_scr[:, lanes] = (mixed * gain_ref[:, lanes]).astype(bf16)
    for copy in copies_w:
        copy.wait()
    wide = lax.broadcasted_iota(jnp.int32, (ROWS, LANES), 1)
    s_scr[...] = jnp.broadcast_to(squares, (TOKENS, LANES))

    def block(b, _):
        x_ = lax.rem(b + x, 2)
        for c_, out_ref in ((c, keep_ref), (1 - c, send_ref)):
            at = rows_at(2 * x_ + c_, ROWS)
            high, low = split(s_scr[at, :], 2)
            tail = jnp.where(wide == 0, high.astype(f32), jnp.where(wide == 1, low.astype(f32), 0.0))
            part = jnp.dot(m_scr[at, :], w_scr[...], preferred_element_type=f32)
            out_ref[b, :, 0:MODEL] = part.astype(out_ref.dtype)
            out_ref[b, :, MODEL:] = tail.astype(out_ref.dtype)
        return 0

    lax.fori_loop(0, 2, block, 0)


def hidden_kernel(own_ref, other_ref, near_ref, far_ref, gain_ref, hidden_ref, first_ref):
    for b, token_ref in enumerate((own_ref, other_ref)):
        total = near_ref[b].astype(f32) + far_ref[1 - b].astype(f32)
        square = total[:, MODEL:MODEL + 1] + total[:, MODEL + 1:MODEL + 2]
        first = token_ref[0:ROWS, :].astype(f32) + total[:, 0:MODEL] * lax.rsqrt(square / INNER + epsilon)
        hidden_ref[b] = rms(first, gain_ref[...].astype(f32)).astype(bf16)
        if b == 0:
            first_ref[...] = first


def project_kernel(at_ref, *refs):
    packs = refs[0:8]
    mine_ref, theirs_ref = refs[8:10]
    q_ref, pack_ref = refs[10:12]
    w_scr, h_scr, sems = refs[12:]
    copies = fetch(views(packs, 0, 64), placed(at_ref, w_scr, 64), sems)
    x, c = at_ref[1], at_ref[2]
    for b, x_ in enumerate((x, 1 - x)):
        h_scr[rows_at(2 * x_ + c, ROWS), :] = mine_ref[b]
        h_scr[rows_at(2 * x_ + 1 - c, ROWS), :] = theirs_ref[b]
    for copy in copies:
        copy.wait()
    out = lax.dot_general(
        h_scr[...], w_scr[...], (((1,), (1,)), ((), ())), preferred_element_type=f32).astype(bf16)
    q_ref[...] = out[:, 0:256]
    pack_ref[...] = out[:, 256:512]


def attend_rows(at_ref, plane, t, k, v, q_ref, start_ref, acc_ref, stat_ref):
    tile = 256
    scale = math.log2(math.e) / math.sqrt(ATTN_DIM)
    rows = rows_at(t, tile)
    column = lax.broadcasted_iota(jnp.int32, (tile, TOKENS), 1)
    low = start_ref[rows, 0:1] - plane * TOKENS
    high = (at_ref[0] - plane) * TOKENS + t * tile + lax.broadcasted_iota(jnp.int32, (tile, 1), 0)
    seen = (column >= low) & (column <= high)
    stat = stat_ref[rows, :]
    lane = lax.broadcasted_iota(jnp.int32, (tile, LANES), 1)
    for h in range(2):
        lanes = pl.ds(h * ATTN_DIM, ATTN_DIM)
        top, total = stat[:, 2 * h:2 * h + 1], stat[:, 2 * h + 1:2 * h + 2]
        s = lax.dot_general(q_ref[rows, lanes], k, (((1,), (1,)), ((), ())), preferred_element_type=f32)
        s = jnp.where(seen, s * scale, -1e30)
        new = jnp.maximum(top, jnp.max(s, axis=1, keepdims=True))
        shift = jnp.exp2(top - new)
        p = jnp.exp2(s - new)
        total = total * shift + jnp.sum(p, axis=1, keepdims=True)
        acc_ref[rows, lanes] = acc_ref[rows, lanes] * shift + jnp.dot(
            p.astype(bf16), v, preferred_element_type=f32)
        stat = jnp.where(lane == 2 * h, new, jnp.where(lane == 2 * h + 1, total, stat))
    stat_ref[rows, :] = stat


def round_kernel(at_ref, block_ref, r_ref, up_ref, down_ref, q_ref, start_ref, acc_in, stat_in, acc_ref, stat_ref, kv_scr):
    z, first, r = at_ref[0], block_ref[0], r_ref[0]

    @pl.when(r == 0)
    def _():
        acc_ref[...] = jnp.zeros_like(acc_ref)
        lane = lax.broadcasted_iota(jnp.int32, stat_ref.shape, 1)
        stat_ref[...] = jnp.where(lane % 2 == 0, -1e29, 0.0)

    @pl.when(r > 0)
    def _():
        acc_ref[...] = acc_in[...]
        stat_ref[...] = stat_in[...]

    kv_scr[0] = up_ref[...]
    kv_scr[1] = down_ref[...]

    def part(n, _):
        side, t = n // 2, lax.rem(n, 2)
        plane = lax.rem(z + PLANES + jnp.where(side == 0, -r, r), PLANES)

        @pl.when((plane >= first) & (plane <= z) & ((side == 0) | (r > 0)))
        def _():
            attend_rows(at_ref, plane, t, kv_scr[side, :, 0:ATTN_DIM], kv_scr[side, :, ATTN_DIM:],
                        q_ref, start_ref, acc_ref, stat_ref)

        return 0

    lax.fori_loop(0, 4, part, 0)


def attend_kernel(at_ref, block_ref, *refs):
    far_ref, weights = refs[0], refs[1:9]
    q_ref, start_ref, acc_ref, stat_ref = refs[9:13]
    keep_ref, send_ref = refs[13:15]
    w_scr, c_scr, a_scr, s_scr, sems = refs[15:]
    z, first = at_ref[0], block_ref[0]
    copies_w = fetch(views(weights, 64, 96), placed(at_ref, w_scr, 32), sems)
    plane = z - PLANES // 2
    a_scr[...] = acc_ref[...]
    s_scr[...] = stat_ref[...]

    @pl.when((plane >= 0) & (plane >= first))
    def _():
        def part(t, _):
            attend_rows(at_ref, plane, t, far_ref[:, 0:ATTN_DIM], far_ref[:, ATTN_DIM:],
                        q_ref, start_ref, a_scr, s_scr)
            return 0

        lax.fori_loop(0, 2, part, 0)

    for h in range(2):
        lanes = pl.ds(h * ATTN_DIM, ATTN_DIM)
        c_scr[:, lanes] = (a_scr[:, lanes] / s_scr[:, 2 * h + 1:2 * h + 2]).astype(bf16)
    for copy in copies_w:
        copy.wait()
    x, c = at_ref[1], at_ref[2]
    for b, x_ in enumerate((x, 1 - x)):
        keep_ref[b] = jnp.dot(c_scr[rows_at(2 * x_ + c, ROWS), :], w_scr[...], preferred_element_type=f32)
        send_ref[b] = jnp.dot(
            c_scr[rows_at(2 * x_ + 1 - c, ROWS), :], w_scr[...], preferred_element_type=f32).astype(bf16)


def layer_pair(tokens, segment_ids, norm_gain, w_mamba_in, w_ssm_param, ssm_rate, dt_bias,
              skip_gain, ssm_norm_gain, w_mamba_out, w_qkv, w_attn_out):
    z, x, c = (lax.axis_index(name) for name in CTX)
    q = 2 * x + c
    at = jnp.stack([z, x, c])
    dma = pltpu.SemaphoreType.DMA

    weights = ring(jnp.transpose(w_mamba_in[0]), None)

    seg_rows = jnp.pad(segment_ids.astype(bf16), ((0, 15), (0, MODEL - ROWS)))
    own = moved(jnp.concatenate([tokens[0], seg_rows]), "blk", lambda i: (i - 1) % 8)
    own, _ = lax.optimization_barrier((own, (weights[2], weights[6])))
    other = swapped(own, "x")
    blocks = [own, other, swapped(own, "c"), swapped(other, "c")]

    heads = 4 * jnp.arange(HEADS) + q
    pick = (heads[:, None] == jnp.arange(32)[None, :]).astype(f32)
    per_head = jnp.stack([dt_bias[0], ssm_rate[0], skip_gain[0]]).astype(f32)
    per_head = jnp.dot(per_head, pick.T, precision=highest)
    head = jnp.pad(per_head[:2], ((0, 6), (0, LANES - HEADS)))
    skip = jnp.repeat(per_head[2], HEAD_DIM)[None, :]
    gain_ssm = jnp.dot(pick, ssm_norm_gain[0].reshape(32, HEAD_DIM).astype(f32), precision=highest)
    gain_ssm = gain_ssm.reshape(1, HEADS * HEAD_DIM)
    w_prm = w_ssm_param[0]
    raw = jnp.dot(w_prm[:, 2 * STATE:], pick.T.astype(bf16), preferred_element_type=f32).astype(bf16)
    w_prm = jnp.concatenate(
        [w_prm[:, STATE:2 * STATE], w_prm[:, :STATE], raw, jnp.zeros((MODEL, LANES - HEADS), bf16)], axis=1)

    order = [(s, (s % 8) * 4 + s // 8) for s in range(32)]
    qkv_slots = []
    for j in range(4):
        mine = [4 * j, 4 * j + 1, 4 * j + 2, 4 * j + 3, 16 + 2 * j, 17 + 2 * j, 24 + 2 * j, 25 + 2 * j]
        qkv_slots += [(s, k * 4 + j) for k, s in enumerate(mine)]
    turned, rows_out, _ = lax.optimization_barrier((jnp.transpose(w_qkv[0]), w_attn_out[0], weights))
    turned = lax.ppermute(turned, CTX, qkv_slots)
    rows_out = lax.ppermute(rows_out, CTX, order)
    later = jnp.concatenate([turned, rows_out])


    u, prm, segc, segr, pack = local(
        enter_kernel,
        [((TOKENS, 512), bf16), ((TOKENS, 256), f32), ((TOKENS, LANES), f32), ((1, TOKENS), f32), ((112, MODEL), bf16)],
        [smem] + [whole] * 12 + [vmem] * 4,
        [pltpu.VMEM((4, ROWS + 16, MODEL), bf16), pltpu.VMEM((512, MODEL), bf16),
         pltpu.VMEM((TOKENS, MODEL), bf16), dma((13,))],
        1 << 30, 6 << 20,
        at, *blocks, *weights, w_mamba_out[0], norm_gain[0, 0:1], w_prm, head)
    packs = ring(pack, 48)

    y, cum = local(
        space_kernel, [((TOKENS, 512), f32), ((TOKENS, LANES), f32)], [vmem] * 6,
        [pltpu.VMEM((STATE, 512), f32)], 1 << 30, 6 << 20,
        u, prm, head, skip, segc, segr)
    y, later = lax.optimization_barrier((y, later))
    keep, send, start, first_block = local(
        leave_kernel,
        [((2, ROWS, MODEL + LANES), f32), ((2, ROWS, MODEL + LANES), bf16), ((TOKENS, LANES), jnp.int32),
         ((1,), jnp.int32)],
        [smem] + [whole] * 9 + [vmem] * 5,
        [pltpu.VMEM((PLANES, 48, MODEL), bf16), pltpu.VMEM((512, MODEL), bf16),
         pltpu.VMEM((TOKENS, 512), bf16), pltpu.VMEM((TOKENS, LANES), f32), dma((16,))],
        1 << 30, 6 << 20,
        at, *packs, y, cum, prm, segc, gain_ssm)
    near = (keep + swapped(send, "c").astype(f32)).astype(bf16)
    far = swapped(near, "x")
    weights = ring(later, None, (send, near, None))
    hidden, first = local(
        hidden_kernel, [((2, ROWS, MODEL), bf16), ((ROWS, MODEL), f32)],
        [vmem] * 5, [], 1 << 20, 2 << 20,
        own, other, near, far, norm_gain[0, 1:2])

    query, pack = local(
        project_kernel, [((TOKENS, 256), bf16), ((TOKENS, 256), bf16)],
        [smem] + [whole] * 8 + [vmem] * 2,
        [pltpu.VMEM((512, MODEL), bf16), pltpu.VMEM((TOKENS, MODEL), bf16), dma((8,))],
        1 << 30, 4 << 20,
        at, *weights, hidden, swapped(hidden, "c"))

    def turn(r, carry):
        up, down, acc, stat = carry
        acc, stat = local(
            round_kernel, [((TOKENS, 256), f32), ((TOKENS, LANES), f32)],
            [smem] * 3 + [vmem] * 6, [pltpu.VMEM((2, TOKENS, 256), bf16)],
            1 << 30, 3 << 20,
            at, first_block, r.reshape(1), up, down, query, start, acc, stat, aliases={7: 0, 8: 1})
        up = moved(up, "z", lambda i: (i + 1) % PLANES)
        down = moved(down, "z", lambda i: (i - 1) % PLANES)
        return up, down, acc, stat

    empty = (jnp.zeros((TOKENS, 256), f32), jnp.zeros((TOKENS, LANES), f32))
    far, _, acc, stat = lax.fori_loop(0, PLANES // 2, turn, (pack, pack, *empty))
    keep, send = local(
        attend_kernel, [((2, ROWS, MODEL), f32), ((2, ROWS, MODEL), bf16)],
        [smem, smem, vmem] + [whole] * 8 + [vmem] * 4,
        [pltpu.VMEM((256, MODEL), bf16), pltpu.VMEM((TOKENS, 256), bf16),
         pltpu.VMEM((TOKENS, 256), f32), pltpu.VMEM((TOKENS, LANES), f32), dma((8,))],
        1 << 30, 6 << 20,
        at, first_block, far, *weights, query, start, acc, stat)
    got = swapped(send, "c").astype(f32)
    mine = (first + keep[0] + got[0]).astype(bf16)
    send = (keep[1] + got[1]).astype(bf16)
    place = lambda i, f: ((i // 4 + 1) % 8) * 4 + f(i % 4)
    straight = [(i, place(i, lambda k: k)) for i in range(32)]
    cross = [(i, place(i, lambda k: k ^ 2)) for i in range(32)]
    mine = lax.ppermute(mine, ("blk", "x", "c"), straight)
    theirs = lax.ppermute(send, ("blk", "x", "c"), cross)
    return (mine.astype(f32) + theirs.astype(f32)).astype(bf16)[None]


def solution(mesh):
    finer = Mesh(mesh.devices.reshape(8, PLANES, 2, 2), ("blk", *CTX))
    rows = lambda *spec: P("blk", *spec)
    in_specs = (
        rows(CTX, None), rows(CTX), rows(None, None), rows(None, CTX), rows(None, None), rows(None),
        rows(None), rows(None), rows(None), rows(CTX, None), rows(None, CTX), rows(CTX, None),
    )
    return jax.shard_map(
        layer_pair, mesh=finer, in_specs=in_specs, out_specs=rows(CTX, None), check_vma=False)
```

time: 564 us -> 198 us (0.35); the launches traced: 556 us -> 197 us
  waiting for transfers between devices: 224 us -> 64.1 us
  local copies, waits for them, and re-layouts: 130 us -> 9.22 us
  starting transfers between devices: 22 us -> 78.4 us
  blocking collectives: 53 us -> 0 us
  between operations: 49.9 us -> 0.52 us
  matrix products: 49.1 us -> 0.56 us
  Pallas kernels: 0 us -> 38.9 us
  other arithmetic: 24.8 us -> 5.23 us
    all_gather x9 -> x0, waiting for transfers between devices: 207 us -> none  [the longest x1 50.5 us: layer_pair(): lax.all_gather(w_mamba_in, CTX, axis=1, tiled=True)]
    ppermute x10 -> x42, starting transfers between devices: 21.7 us -> 78.4 us  [the longest x38 66.6 us: moved(): return lax.ppermute(value, axis, [(i, target(i)) for i in range(count)])]
    dynamic_update_slice x2 -> x0, local copies, waits for them, and re-layouts: 50.9 us -> none  [layer_pair(): (local_state, ignored), mixed = lax.scan(span_update, start_carry, blocks)]
    dot_general x16 -> x3, matrix products: 49.1 us -> 0.56 us  [the longest x1 0.19 us: layer_pair(): jnp.dot(w_prm[:, 2 * STATE:], pick.T.astype(bf16), preferred_element_type...]
    ppermute x10 -> x42, waiting for transfers between devices: 17 us -> 64.1 us  [the longest x38 46.5 us: moved(): return lax.ppermute(value, axis, [(i, target(i)) for i in range(count)])]
    pallas_call x0 -> x10, Pallas kernels: none -> 38.9 us  [local(): pl.pallas_call(kernel, out_shape=tuple((jax.ShapeDtypeStruct(shape, kind)...]
    all_gather x2 -> x0, blocking collectives: 37.2 us -> none  [the longest x1 32.6 us: layer_pair(): lax.all_gather(segment, CTX, axis=0, tiled=True)]
    squeeze x18 -> x2, local copies, waits for them, and re-layouts: 21.5 us -> 0.61 us  [the longest x1 0.61 us: layer_pair(): norm_gain[0, 1:2]]
  transfers between devices with their start and end apart: 19 -> 42, of which waited for: 10 -> 23; matrix products, arithmetic and copies ran while one was open for 20% -> 4% of each run, Pallas kernels for 0% -> 9%
where the time goes in v1:
time: 198 us; the launch traced here: 197 us
  starting transfers between devices  78.4 us (40%)
  waiting for transfers between devices  64.1 us (32%)
  Pallas kernels  38.9 us (20%)
  local copies, waits for them, and re-layouts  9.22 us (5%)
  other arithmetic  5.23 us (3%)
    ppermute x38, starting transfers between devices, moved(): return lax.ppermute(value, axis, [(i, target(i)) for i in range(count)])  66.6 us
    ppermute x38, waiting for transfers between devices, moved(): return lax.ppermute(value, axis, [(i, target(i)) for i in range(count)])  46.5 us
    pallas_call x10, Pallas kernels, local(): pl.pallas_call(kernel, out_shape=tuple((jax.ShapeDtypeStruct(shape, kind)...  38.9 us
    ppermute x1, waiting for transfers between devices, layer_pair(): mine = lax.ppermute(mine, ('blk', 'x', 'c'), straight)  10.3 us
    ppermute x1, starting transfers between devices, layer_pair(): turned = lax.ppermute(turned, CTX, qkv_slots)  8.94 us
    ppermute x1, waiting for transfers between devices, layer_pair(): theirs = lax.ppermute(send, ('blk', 'x', 'c'), cross)  6.31 us
    unnamed x82, local copies, waits for them, and re-layouts  5.85 us
  transfers between devices with their start and end apart: 42, of which 23 were waited for; matrix products, arithmetic and copies ran while one was open for 4% of the time, Pallas kernels for 9%

profile of v1, /device:TPU:1, one launch (start us, length us, event | category | flops | bytes accessed | tf_op | source)
XLA Modules:
  0.0 197.1 jit_solution(2160785197671311168)
XLA Ops:
  0.0 6.4 %collective-permute-start.3 = (bf16[64,1024]{1,0:T(8,128)(2,1)}, bf16[64,1024]{1,0:T(8,128)(2,1)S(1)}, u32[]{:S(2)}, u32[]{:S(2)}) collective-permute-start(bf16[64,1024]{1,0:T(8,128)(2,1)} %bitcast.42), channel_id=1, source_target_pairs={{0,28},{4,0},{8,4},{12,8},{16,12},{20,16},{24,20},{28,24},{1,29},{... | collective-permute-start | bytes 393224 | tf_op jit(solution)/shard_map/ppermute | solution.py:31
  8.0 5.3 %collective-permute-start.2 = (bf16[144,1024]{1,0:T(8,128)(2,1)S(1)}, bf16[144,1024]{1,0:T(8,128)(2,1)S(1)}, u32[]{:S(2)}, u32[]{:S(2)}) collective-permute-start(bf16[144,1024]{1,0:T(8,128)(2,1)S(1)} %fusion.4), channel_id=1, source_target_pairs={{0,224},{32,0},{64,32},{96,64},{128,96},{160,128},{192,160},{224,1... | collective-permute-start | bytes 884744 | tf_op jit(solution)/shard_map/ppermute | solution.py:31
  15.0 2.7 %collective-permute-start.4 = (bf16[64,1024]{1,0:T(8,128)(2,1)S(1)}, bf16[64,1024]{1,0:T(8,128)(2,1)S(1)}, u32[]{:S(2)}, u32[]{:S(2)}) collective-permute-start(bf16[64,1024]{1,0:T(8,128)(2,1)S(1)} %collective-permute-done.3.refs_5_), channel_id=1, source_target_pairs={{0,28},{4,0},{8,4},{12,8},{16,12},{20,16},{24,20},{28,24},{1,29},{... | collective-permute-start | bytes 393224 | tf_op jit(solution)/shard_map/ppermute | solution.py:31
  17.9 1.8 collective-permute-done.4.refs_6_
  19.7 3.1 %collective-permute-done.6.refs_10_ = bf16[64,1024]{1,0:T(8,128)(2,1)S(1)} collective-permute-done((bf16[64,1024]{1,0:T(8,128)(2,1)S(1)}, bf16[64,1024]{1,0:T(8,128)(2,1)S(1)}, u32[]{:S(2)}, u32[]{:S(2)}) %collective-permute-start.6) | collective-permute-done | bytes 131104 | tf_op jit(solution)/shard_map/ppermute | solution.py:31
  24.9 2.7 %collective-permute-start.10 = (bf16[64,1024]{1,0:T(8,128)(2,1)S(1)}, bf16[64,1024]{1,0:T(8,128)(2,1)S(1)}, u32[]{:S(2)}, u32[]{:S(2)}) collective-permute-start(bf16[64,1024]{1,0:T(8,128)(2,1)S(1)} %collective-permute-done.4.refs_6_), channel_id=1, source_target_pairs={{0,28},{4,0},{8,4},{12,8},{16,12},{20,16},{24,20},{28,24},{1,29},{... | collective-permute-start | bytes 393224 | tf_op jit(solution)/shard_map/ppermute | solution.py:31
  27.6 3.8 %collective-permute-start.8 = (bf16[144,1024]{1,0:T(8,128)(2,1)S(1)}, bf16[144,1024]{1,0:T(8,128)(2,1)S(1)}, u32[]{:S(2)}, u32[]{:S(2)}) collective-permute-start(bf16[144,1024]{1,0:T(8,128)(2,1)S(1)} %collective-permute-done.2.refs_0_.own_ref), channel_id=1, source_target_pairs={{0,1},{1,0},{2,3},{3,2},{4,5},{5,4},{6,7},{7,6},{8,9},{9,8},{10,11... | collective-permute-start | bytes 884744 | tf_op jit(solution)/shard_map/ppermute | solution.py:31
  31.4 2.4 %collective-permute-start.9 = (bf16[144,1024]{1,0:T(8,128)(2,1)S(1)}, bf16[144,1024]{1,0:T(8,128)(2,1)S(1)}, u32[]{:S(2)}, u32[]{:S(2)}) collective-permute-start(bf16[144,1024]{1,0:T(8,128)(2,1)S(1)} %collective-permute-done.7.refs_1_.other_ref), channel_id=1, source_target_pairs={{0,1},{1,0},{2,3},{3,2},{4,5},{5,4},{6,7},{7,6},{8,9},{9,8},{10,11... | collective-permute-start | bytes 884744 | tf_op jit(solution)/shard_map/ppermute | solution.py:31
  34.7 1.7 collective-permute-done.12.refs_8_
  37.3 6.0 %shard_map.118 = (bf16[512,512]{1,0:T(8,128)(2,1)}, f32[512,256]{1,0:T(8,128)}, f32[512,128]{1,0:T(8,128)}, f32[1,512]{1,0:T(1,128)}, bf16[112,1024]{1,0:T(8,128)(2,1)}) custom-call(s32[3]{0:T(128)S(1)} %pad_add_fusion.at_ref, bf16[144,1024]{1,0:T(8,128)(2,1)} %copy-done.6, bf16[144,1024]{1,0:T(8,128)(2,1)} %copy-done.7, bf16[144,1024]{1,0:T(8,128)(2,1)} %copy-done.14, ...), custom_call_target="tpu_custom_call" | custom-call | flops 1073741824 | bytes 6291456 | tf_op jit(solution)/shard_map/pallas_call | solution.py:66
  44.9 3.6 %collective-permute-done.13.refs_1_ = bf16[112,1024]{1,0:T(8,128)(2,1)S(1)} collective-permute-done((bf16[112,1024]{1,0:T(8,128)(2,1)}, bf16[112,1024]{1,0:T(8,128)(2,1)S(1)}, u32[]{:S(2)}, u32[]{:S(2)}) %collective-permute-start.13) | collective-permute-done | bytes 229408 | tf_op jit(solution)/shard_map/ppermute | solution.py:31
  48.5 2.9 %collective-permute-start.14 = (bf16[112,1024]{1,0:T(8,128)(2,1)S(1)}, bf16[112,1024]{1,0:T(8,128)(2,1)S(1)}, u32[]{:S(2)}, u32[]{:S(2)}) collective-permute-start(bf16[112,1024]{1,0:T(8,128)(2,1)S(1)} %collective-permute-done.13.refs_1_), channel_id=1, source_target_pairs={{0,28},{4,0},{8,4},{12,8},{16,12},{20,16},{24,20},{28,24},{1,29},{... | collective-permute-start | bytes 688136 | tf_op jit(solution)/shard_map/ppermute | solution.py:31
  51.5 3.3 %collective-permute-done.14.refs_2_ = bf16[112,1024]{1,0:T(8,128)(2,1)S(1)} collective-permute-done((bf16[112,1024]{1,0:T(8,128)(2,1)S(1)}, bf16[112,1024]{1,0:T(8,128)(2,1)S(1)}, u32[]{:S(2)}, u32[]{:S(2)}) %collective-permute-start.14) | collective-permute-done | bytes 229408 | tf_op jit(solution)/shard_map/ppermute | solution.py:31
  54.9 2.6 %collective-permute-start.15 = (bf16[112,1024]{1,0:T(8,128)(2,1)S(1)}, bf16[112,1024]{1,0:T(8,128)(2,1)S(1)}, u32[]{:S(2)}, u32[]{:S(2)}) collective-permute-start(bf16[112,1024]{1,0:T(8,128)(2,1)S(1)} %collective-permute-done.14.refs_2_), channel_id=1, source_target_pairs={{0,28},{4,0},{8,4},{12,8},{16,12},{20,16},{24,20},{28,24},{1,29},{... | collective-permute-start | bytes 688136 | tf_op jit(solution)/shard_map/ppermute | solution.py:31
  57.7 8.9 %collective-permute-start.21 = (bf16[64,1024]{1,0:T(8,128)(2,1)S(1)}, bf16[64,1024]{1,0:T(8,128)(2,1)S(1)}, u32[]{:S(2)}, u32[]{:S(2)}) collective-permute-start(bf16[64,1024]{1,0:T(8,128)(2,1)S(1)} %bitcast.46), channel_id=1, source_target_pairs={{0,0},{1,4},{2,8},{3,12},{16,16},{17,20},{24,24},{25,28},{4,1},{5,... | collective-permute-start | bytes 393224 | tf_op jit(solution)/shard_map/ppermute | solution.py:479
  66.6 1.9 collective-permute-start.22
  68.6 2.1 %collective-permute-start.18 = (bf16[112,1024]{1,0:T(8,128)(2,1)S(1)}, bf16[112,1024]{1,0:T(8,128)(2,1)S(1)}, u32[]{:S(2)}, u32[]{:S(2)}) collective-permute-start(bf16[112,1024]{1,0:T(8,128)(2,1)S(1)} %collective-permute-done.17.refs_7_), channel_id=1, source_target_pairs={{0,4},{4,8},{8,12},{12,16},{16,20},{20,24},{24,28},{28,0},{1,5},{5... | collective-permute-start | bytes 688136 | tf_op jit(solution)/shard_map/ppermute | solution.py:31
  73.9 1.6 collective-permute-done.18.refs_6_
  77.0 6.1 %shard_map.119 = (f32[512,512]{1,0:T(8,128)}, f32[512,128]{1,0:T(8,128)}) custom-call(bf16[512,512]{1,0:T(8,128)(2,1)} %get-tuple-element.175.u_ref, f32[512,256]{1,0:T(8,128)} %get-tuple-element.176.prm_ref.refs_11_, f32[8,128]{1,0:T(8,128)} %pad.9.refs_15_.head_ref, f32[1,512]{1,0:T(1,128)} %broadcast_in_dim_reshape.3.skip_ref, ...), custom_call_target="tpu_custom_call" | custom-call | flops 1073741824 | bytes 6291456 | tf_op jit(solution)/shard_map/pallas_call | solution.py:66
  83.8 6.4 %shard_map.120 = (f32[2,128,1152]{2,1,0:T(8,128)}, bf16[2,128,1152]{2,1,0:T(8,128)(2,1)}, s32[512,128]{1,0:T(8,128)S(1)}, s32[1]{0:T(128)}) custom-call(s32[3]{0:T(128)S(1)} %pad_add_fusion.at_ref, bf16[112,1024]{1,0:T(8,128)(2,1)} %get-tuple-element.174.refs_0_, bf16[112,1024]{1,0:T(8,128)(2,1)} %copy-done.16, bf16[112,1024]{1,0:T(8,128)(2,1)} %copy-done.18, ...), custom_call_target="tpu_custom_call" | custom-call | flops 1073741824 | bytes 6291456 | tf_op jit(solution)/shard_map/pallas_call | solution.py:66
  90.5 2.0 %collective-permute-done.23 = bf16[2,128,1152]{2,1,0:T(8,128)(2,1)S(1)} collective-permute-done((bf16[2,128,1152]{2,1,0:T(8,128)(2,1)}, bf16[2,128,1152]{2,1,0:T(8,128)(2,1)S(1)}, u32[]{:S(2)}, u32[]{:S(2)}) %collective-permute-start.23) | collective-permute-done | bytes 589856 | tf_op jit(solution)/shard_map/ppermute | solution.py:31
  93.9 3.1 %collective-permute-start.24 = (bf16[2,128,1152]{2,1,0:T(8,128)(2,1)S(1)}, bf16[2,128,1152]{2,1,0:T(8,128)(2,1)S(1)}, u32[]{:S(2)}, u32[]{:S(2)}) collective-permute-start(bf16[2,128,1152]{2,1,0:T(8,128)(2,1)S(1)} %add_convert_fusion.near_ref), channel_id=1, source_target_pairs={{0,2},{2,0},{1,3},{3,1},{4,6},{6,4},{5,7},{7,5},{8,10},{10,8},{9,1... | collective-permute-start | bytes 1769480 | tf_op jit(solution)/shard_map/ppermute | solution.py:31
  97.0 1.6 collective-permute-start.25
  99.6 4.3 %collective-permute-done.25.refs_7_.refs_8_ = bf16[96,1024]{1,0:T(8,128)(2,1)S(1)} collective-permute-done((bf16[96,1024]{1,0:T(8,128)(2,1)S(1)}, bf16[96,1024]{1,0:T(8,128)(2,1)S(1)}, u32[]{:S(2)}, u32[]{:S(2)}) %collective-permute-start.25) | collective-permute-done | bytes 196640 | tf_op jit(solution)/shard_map/ppermute | solution.py:31
  106.8 3.5 %collective-permute-done.24.far_ref = bf16[2,128,1152]{2,1,0:T(8,128)(2,1)S(1)} collective-permute-done((bf16[2,128,1152]{2,1,0:T(8,128)(2,1)S(1)}, bf16[2,128,1152]{2,1,0:T(8,128)(2,1)S(1)}, u32[]{:S(2)}, u32[]{:S(2)}) %collective-permute-start.24) | collective-permute-done | bytes 589856 | tf_op jit(solution)/shard_map/ppermute | solution.py:31
  111.1 2.7 %shard_map.121 = (bf16[2,128,1024]{2,1,0:T(8,128)(2,1)}, f32[128,1024]{1,0:T(8,128)}) custom-call(bf16[144,1024]{1,0:T(8,128)(2,1)} %copy-done.6, bf16[144,1024]{1,0:T(8,128)(2,1)} %copy-done.7, bf16[2,128,1152]{2,1,0:T(8,128)(2,1)} %copy-done.2, bf16[2,128,1152]{2,1,0:T(8,128)(2,1)} %copy-done.4, bf16[1,1024]{1,0:T(2,128)(2,1)} %get-tuple-element.222.gain_ref), custom_call_target="tpu_custom_call" | custom-call | flops 1048576 | bytes 2097152 | tf_op jit(solution)/shard_map/pallas_call | solution.py:66
  114.8 1.7 collective-permute-start.30
  117.5 5.0 %collective-permute-done.30.refs_5_.refs_6_ = bf16[96,1024]{1,0:T(8,128)(2,1)S(1)} collective-permute-done((bf16[96,1024]{1,0:T(8,128)(2,1)S(1)}, bf16[96,1024]{1,0:T(8,128)(2,1)S(1)}, u32[]{:S(2)}, u32[]{:S(2)}) %collective-permute-start.30) | collective-permute-done | bytes 196640 | tf_op jit(solution)/shard_map/ppermute | solution.py:31
  122.9 6.4 %collective-permute-done.31.refs_4_.refs_5_ = bf16[96,1024]{1,0:T(8,128)(2,1)S(1)} collective-permute-done((bf16[96,1024]{1,0:T(8,128)(2,1)S(1)}, bf16[96,1024]{1,0:T(8,128)(2,1)S(1)}, u32[]{:S(2)}, u32[]{:S(2)}) %collective-permute-start.31) | collective-permute-done | bytes 196640 | tf_op jit(solution)/shard_map/ppermute | solution.py:31
  130.8 4.0 %shard_map.122 = (bf16[512,256]{1,0:T(8,128)(2,1)}, bf16[512,256]{1,0:T(8,128)(2,1)S(1)}) custom-call(s32[3]{0:T(128)S(1)} %pad_add_fusion.at_ref, bf16[96,1024]{1,0:T(8,128)(2,1)} %copy-done.8, bf16[96,1024]{1,0:T(8,128)(2,1)} %copy-done.21, bf16[96,1024]{1,0:T(8,128)(2,1)} %copy-done.23, bf16[96,1024]{1,0:T(8,128)(2,1)} %copy-done.25, ...), custom_call_target="tpu_custom_call" | custom-call | flops 1073741824 | bytes 4194304 | tf_op jit(solution)/shard_map/pallas_call | solution.py:66
  135.8 29.7 %while.19 = (s32[]{:T(128)}, bf16[512,256]{1,0:T(8,128)(2,1)S(1)}, bf16[512,256]{1,0:T(8,128)(2,1)S(1)}, f32[512,256]{1,0:T(8,128)S(1)}, f32[512,128]{1,0:T(8,12...) while((s32[]{:T(128)}, bf16[512,256]{1,0:T(8,128)(2,1)S(1)}, ...), condition=%wide.region_1.2_spmd, body=%wide.region_0.1_spmd.sunk | while | flops 1073741824 | bytes 8388853 | solution.py:535
  135.9 2.7 %collective-permute-start.1 = (bf16[512,256]{1,0:T(8,128)(2,1)S(1)}, bf16[512,256]{1,0:T(8,128)(2,1)S(1)}, u32[]{:S(2)}, u32[]{:S(2)}) collective-permute-start(bf16[512,256]{1,0:T(8,128)(2,1)S(1)} %copy.28.down_ref), channel_id=1, source_target_pairs={{0,28},{4,0},{8,4},{12,8},{16,12},{20,16},{24,20},{28,24},{1,29},{... | collective-permute-start | bytes 786440 | tf_op jit(solution)/shard_map/while/body/eval_jaxpr/ppermute | solution.py:31
  138.7 4.1 %eval_jaxpr.5 = (f32[512,256]{1,0:T(8,128)S(1)}, f32[512,128]{1,0:T(8,128)S(1)}) custom-call(s32[3]{0:T(128)S(1)} %get-tuple-element.308.at_ref, s32[1]{0:T(128)} %get-tuple-element.309.block_ref, s32[1]{0:T(128)} %bitcast.37.r_ref, bf16[512,256]{1,0:T(8,128)(2,1)} %copy-done, ...), custom_call_target="tpu_custom_call", output_to_operand_aliasing={{0}: (7, {}), {1}: (8, {})} | custom-call | flops 1073741824 | bytes 3145728 | tf_op jit(solution)/shard_map/while/body/eval_jaxpr/pallas_call | solution.py:66
  143.7 2.4 %collective-permute-start.1 = (bf16[512,256]{1,0:T(8,128)(2,1)S(1)}, bf16[512,256]{1,0:T(8,128)(2,1)S(1)}, u32[]{:S(2)}, u32[]{:S(2)}) collective-permute-start(bf16[512,256]{1,0:T(8,128)(2,1)S(1)} %copy.28.down_ref), channel_id=1, source_target_pairs={{0,28},{4,0},{8,4},{12,8},{16,12},{20,16},{24,20},{28,24},{1,29},{... | collective-permute-start | bytes 786440 | tf_op jit(solution)/shard_map/while/body/eval_jaxpr/ppermute | solution.py:31
  146.1 1.9 eval_jaxpr.5
  148.0 1.8 collective-permute-done
  150.4 2.2 %collective-permute-start = (bf16[512,256]{1,0:T(8,128)(2,1)S(1)}, bf16[512,256]{1,0:T(8,128)(2,1)S(1)}, u32[]{:S(2)}, u32[]{:S(2)}) collective-permute-start(bf16[512,256]{1,0:T(8,128)(2,1)S(1)} %copy.27.up_ref), channel_id=1, source_target_pairs={{0,4},{4,8},{8,12},{12,16},{16,20},{20,24},{24,28},{28,0},{1,5},{5... | collective-permute-start | bytes 786440 | tf_op jit(solution)/shard_map/while/body/eval_jaxpr/ppermute | solution.py:31
  153.3 1.9 eval_jaxpr.5
  155.2 1.7 collective-permute-done
  156.9 1.6 collective-permute-done.1
  158.6 1.5 collective-permute-start
  161.4 1.9 eval_jaxpr.5
  163.3 1.8 collective-permute-done
  165.5 3.8 %shard_map.123 = (f32[2,128,1024]{2,1,0:T(8,128)}, bf16[2,128,1024]{2,1,0:T(8,128)(2,1)}) custom-call(s32[3]{0:T(128)S(1)} %get-tuple-element.339, s32[1]{0:T(128)} %get-tuple-element.289.block_ref, bf16[512,256]{1,0:T(8,128)(2,1)S(1)} %get-tuple-element.197.refs_0_, bf16[96,1024]{1,0:T(8,128)(2,1)} %copy-done.8, bf16[96,1024]{1,0:T(8,128)(2,1)} %copy-done.21, ...), custom_call_target="tpu_custom_call" | custom-call | flops 1073741824 | bytes 6291456 | tf_op jit(solution)/shard_map/pallas_call | solution.py:66
  169.4 7.4 %collective-permute-start.33 = (bf16[2,128,1024]{2,1,0:T(8,128)(2,1)}, bf16[2,128,1024]{2,1,0:T(8,128)(2,1)S(1)}, u32[]{:S(2)}, u32[]{:S(2)}) collective-permute-start(bf16[2,128,1024]{2,1,0:T(8,128)(2,1)} %get-tuple-element.201), channel_id=1, source_target_pairs={{0,1},{1,0},{2,3},{3,2},{4,5},{5,4},{6,7},{7,6},{8,9},{9,8},{10,11... | collective-permute-start | bytes 1572872 | tf_op jit(solution)/shard_map/ppermute | solution.py:31
  176.8 1.7 collective-permute-done.33
  179.7 10.3 %collective-permute-done.34 = bf16[128,1024]{1,0:T(8,128)(2,1)S(1)} collective-permute-done((bf16[128,1024]{1,0:T(8,128)(2,1)S(1)}, bf16[128,1024]{1,0:T(8,128)(2,1)S(1)}, u32[]{:S(2)}, u32[]{:S(2)}) %collective-permute-start.34) | collective-permute-done | bytes 262176 | tf_op jit(solution)/shard_map/ppermute | solution.py:549
  190.1 6.3 %collective-permute-done.35 = bf16[128,1024]{1,0:T(8,128)(2,1)S(1)} collective-permute-done((bf16[128,1024]{1,0:T(8,128)(2,1)S(1)}, bf16[128,1024]{1,0:T(8,128)(2,1)S(1)}, u32[]{:S(2)}, u32[]{:S(2)}) %collective-permute-start.35) | collective-permute-done | bytes 262176 | tf_op jit(solution)/shard_map/ppermute | solution.py:550
  (184 shorter events, 31.7 us)
Async XLA Ops:
  0.0 15.0 %collective-permute-start.3 = (bf16[64,1024]{1,0:T(8,128)(2,1)}, bf16[64,1024]{1,0:T(8,128)(2,1)S(1)}, u32[]{:S(2)}, u32[]{:S(2)}) collective-permute-start(bf16[64,1024]{1,0:T(8,128)(2,1)} %bitcast.42), channel_id=1, source_target_pairs={{0,28},{4,0},{8,4},{12,8},{16,12},{20,16},{24,20},{28,24},{1,29},{... | collective-permute-start | bytes 393224 | tf_op jit(solution)/shard_map/ppermute | solution.py:31
  6.4 11.4 %collective-permute-start.5 = (bf16[64,1024]{1,0:T(8,128)(2,1)}, bf16[64,1024]{1,0:T(8,128)(2,1)S(1)}, u32[]{:S(2)}, u32[]{:S(2)}) collective-permute-start(bf16[64,1024]{1,0:T(8,128)(2,1)} %bitcast.43), channel_id=1, source_target_pairs={{0,4},{4,8},{8,12},{12,16},{16,20},{20,24},{24,28},{28,0},{1,5},{5... | collective-permute-start | bytes 393224 | tf_op jit(solution)/shard_map/ppermute | solution.py:31
  8.0 14.8 %collective-permute-start.2 = (bf16[144,1024]{1,0:T(8,128)(2,1)S(1)}, bf16[144,1024]{1,0:T(8,128)(2,1)S(1)}, u32[]{:S(2)}, u32[]{:S(2)}) collective-permute-start(bf16[144,1024]{1,0:T(8,128)(2,1)S(1)} %fusion.4), channel_id=1, source_target_pairs={{0,224},{32,0},{64,32},{96,64},{128,96},{160,128},{192,160},{224,1... | collective-permute-start | bytes 884744 | tf_op jit(solution)/shard_map/ppermute | solution.py:31
  15.0 4.7 %collective-permute-start.4 = (bf16[64,1024]{1,0:T(8,128)(2,1)S(1)}, bf16[64,1024]{1,0:T(8,128)(2,1)S(1)}, u32[]{:S(2)}, u32[]{:S(2)}) collective-permute-start(bf16[64,1024]{1,0:T(8,128)(2,1)S(1)} %collective-permute-done.3.refs_5_), channel_id=1, source_target_pairs={{0,28},{4,0},{8,4},{12,8},{16,12},{20,16},{24,20},{28,24},{1,29},{... | collective-permute-start | bytes 393224 | tf_op jit(solution)/shard_map/ppermute | solution.py:31
  17.8 5.0 %collective-permute-start.6 = (bf16[64,1024]{1,0:T(8,128)(2,1)S(1)}, bf16[64,1024]{1,0:T(8,128)(2,1)S(1)}, u32[]{:S(2)}, u32[]{:S(2)}) collective-permute-start(bf16[64,1024]{1,0:T(8,128)(2,1)S(1)} %collective-permute-done.5.refs_11_), channel_id=1, source_target_pairs={{0,4},{4,8},{8,12},{12,16},{16,20},{20,24},{24,28},{28,0},{1,5},{5... | collective-permute-start | bytes 393224 | tf_op jit(solution)/shard_map/ppermute | solution.py:31
  22.8 8.6 %collective-permute-start.7 = (bf16[144,1024]{1,0:T(8,128)(2,1)S(1)}, bf16[144,1024]{1,0:T(8,128)(2,1)S(1)}, u32[]{:S(2)}, u32[]{:S(2)}) collective-permute-start(bf16[144,1024]{1,0:T(8,128)(2,1)S(1)} %collective-permute-done.2.refs_0_.own_ref), channel_id=1, source_target_pairs={{0,2},{2,0},{1,3},{3,1},{4,6},{6,4},{5,7},{7,5},{8,10},{10,8},{9,1... | collective-permute-start | bytes 884744 | tf_op jit(solution)/shard_map/ppermute | solution.py:31
  24.3 7.1 %collective-permute-start.11 = (bf16[64,1024]{1,0:T(8,128)(2,1)S(1)}, bf16[64,1024]{1,0:T(8,128)(2,1)S(1)}, u32[]{:S(2)}, u32[]{:S(2)}) collective-permute-start(bf16[64,1024]{1,0:T(8,128)(2,1)S(1)} %collective-permute-done.6.refs_10_), channel_id=1, source_target_pairs={{0,4},{4,8},{8,12},{12,16},{16,20},{20,24},{24,28},{28,0},{1,5},{5... | collective-permute-start | bytes 393224 | tf_op jit(solution)/shard_map/ppermute | solution.py:31
  24.9 9.8 %collective-permute-start.10 = (bf16[64,1024]{1,0:T(8,128)(2,1)S(1)}, bf16[64,1024]{1,0:T(8,128)(2,1)S(1)}, u32[]{:S(2)}, u32[]{:S(2)}) collective-permute-start(bf16[64,1024]{1,0:T(8,128)(2,1)S(1)} %collective-permute-done.4.refs_6_), channel_id=1, source_target_pairs={{0,28},{4,0},{8,4},{12,8},{16,12},{20,16},{24,20},{28,24},{1,29},{... | collective-permute-start | bytes 393224 | tf_op jit(solution)/shard_map/ppermute | solution.py:31
  27.6 8.8 %collective-permute-start.8 = (bf16[144,1024]{1,0:T(8,128)(2,1)S(1)}, bf16[144,1024]{1,0:T(8,128)(2,1)S(1)}, u32[]{:S(2)}, u32[]{:S(2)}) collective-permute-start(bf16[144,1024]{1,0:T(8,128)(2,1)S(1)} %collective-permute-done.2.refs_0_.own_ref), channel_id=1, source_target_pairs={{0,1},{1,0},{2,3},{3,2},{4,5},{5,4},{6,7},{7,6},{8,9},{9,8},{10,11... | collective-permute-start | bytes 884744 | tf_op jit(solution)/shard_map/ppermute | solution.py:31
  31.4 5.0 %collective-permute-start.12 = (bf16[64,1024]{1,0:T(8,128)(2,1)S(1)}, bf16[64,1024]{1,0:T(8,128)(2,1)S(1)}, u32[]{:S(2)}, u32[]{:S(2)}) collective-permute-start(bf16[64,1024]{1,0:T(8,128)(2,1)S(1)} %collective-permute-done.11.refs_9_), channel_id=1, source_target_pairs={{0,4},{4,8},{8,12},{12,16},{16,20},{20,24},{24,28},{28,0},{1,5},{5... | collective-permute-start | bytes 393224 | tf_op jit(solution)/shard_map/ppermute | solution.py:31
  31.4 5.0 %collective-permute-start.9 = (bf16[144,1024]{1,0:T(8,128)(2,1)S(1)}, bf16[144,1024]{1,0:T(8,128)(2,1)S(1)}, u32[]{:S(2)}, u32[]{:S(2)}) collective-permute-start(bf16[144,1024]{1,0:T(8,128)(2,1)S(1)} %collective-permute-done.7.refs_1_.other_ref), channel_id=1, source_target_pairs={{0,1},{1,0},{2,3},{3,2},{4,5},{5,4},{6,7},{7,6},{8,9},{9,8},{10,11... | collective-permute-start | bytes 884744 | tf_op jit(solution)/shard_map/ppermute | solution.py:31
  37.3 29.4 %copy-start.37 = (bf16[1,32,1024]{2,1,0:T(8,128)(2,1)S(1)}, bf16[1,32,1024]{2,1,0:T(8,128)(2,1)}, u32[]{:S(2)}) copy-start(bf16[1,32,1024]{2,1,0:T(8,128)(2,1)} %param.25) | copy-start | bytes 196612
  43.3 5.2 %collective-permute-start.13 = (bf16[112,1024]{1,0:T(8,128)(2,1)}, bf16[112,1024]{1,0:T(8,128)(2,1)S(1)}, u32[]{:S(2)}, u32[]{:S(2)}) collective-permute-start(bf16[112,1024]{1,0:T(8,128)(2,1)} %get-tuple-element.174.refs_0_), channel_id=1, source_target_pairs={{0,28},{4,0},{8,4},{12,8},{16,12},{20,16},{24,20},{28,24},{1,29},{... | collective-permute-start | bytes 688136 | tf_op jit(solution)/shard_map/ppermute | solution.py:31
  44.7 6.7 %collective-permute-start.16 = (bf16[112,1024]{1,0:T(8,128)(2,1)}, bf16[112,1024]{1,0:T(8,128)(2,1)S(1)}, u32[]{:S(2)}, u32[]{:S(2)}) collective-permute-start(bf16[112,1024]{1,0:T(8,128)(2,1)} %get-tuple-element.174.refs_0_), channel_id=1, source_target_pairs={{0,4},{4,8},{8,12},{12,16},{16,20},{20,24},{24,28},{28,0},{1,5},{5... | collective-permute-start | bytes 688136 | tf_op jit(solution)/shard_map/ppermute | solution.py:31
  48.5 34.6 %copy-start.16 = (bf16[112,1024]{1,0:T(8,128)(2,1)}, bf16[112,1024]{1,0:T(8,128)(2,1)S(1)}, u32[]{:S(2)}) copy-start(bf16[112,1024]{1,0:T(8,128)(2,1)S(1)} %collective-permute-done.13.refs_1_) | copy-start | bytes 688132
  48.5 6.4 %collective-permute-start.14 = (bf16[112,1024]{1,0:T(8,128)(2,1)S(1)}, bf16[112,1024]{1,0:T(8,128)(2,1)S(1)}, u32[]{:S(2)}, u32[]{:S(2)}) collective-permute-start(bf16[112,1024]{1,0:T(8,128)(2,1)S(1)} %collective-permute-done.13.refs_1_), channel_id=1, source_target_pairs={{0,28},{4,0},{8,4},{12,8},{16,12},{20,16},{24,20},{28,24},{1,29},{... | collective-permute-start | bytes 688136 | tf_op jit(solution)/shard_map/ppermute | solution.py:31
  51.4 31.6 %copy-start.17 = (bf16[112,1024]{1,0:T(8,128)(2,1)}, bf16[112,1024]{1,0:T(8,128)(2,1)S(1)}, u32[]{:S(2)}) copy-start(bf16[112,1024]{1,0:T(8,128)(2,1)S(1)} %collective-permute-done.16.refs_8_) | copy-start | bytes 688132
  51.4 17.2 %collective-permute-start.17 = (bf16[112,1024]{1,0:T(8,128)(2,1)S(1)}, bf16[112,1024]{1,0:T(8,128)(2,1)S(1)}, u32[]{:S(2)}, u32[]{:S(2)}) collective-permute-start(bf16[112,1024]{1,0:T(8,128)(2,1)S(1)} %collective-permute-done.16.refs_8_), channel_id=1, source_target_pairs={{0,4},{4,8},{8,12},{12,16},{16,20},{20,24},{24,28},{28,0},{1,5},{5... | collective-permute-start | bytes 688136 | tf_op jit(solution)/shard_map/ppermute | solution.py:31
  54.9 28.2 %copy-start.18 = (bf16[112,1024]{1,0:T(8,128)(2,1)}, bf16[112,1024]{1,0:T(8,128)(2,1)S(1)}, u32[]{:S(2)}) copy-start(bf16[112,1024]{1,0:T(8,128)(2,1)S(1)} %collective-permute-done.14.refs_2_) | copy-start | bytes 688132
  54.9 17.2 %collective-permute-start.15 = (bf16[112,1024]{1,0:T(8,128)(2,1)S(1)}, bf16[112,1024]{1,0:T(8,128)(2,1)S(1)}, u32[]{:S(2)}, u32[]{:S(2)}) collective-permute-start(bf16[112,1024]{1,0:T(8,128)(2,1)S(1)} %collective-permute-done.14.refs_2_), channel_id=1, source_target_pairs={{0,28},{4,0},{8,4},{12,8},{16,12},{20,16},{24,20},{28,24},{1,29},{... | collective-permute-start | bytes 688136 | tf_op jit(solution)/shard_map/ppermute | solution.py:31
  57.7 16.2 %collective-permute-start.21 = (bf16[64,1024]{1,0:T(8,128)(2,1)S(1)}, bf16[64,1024]{1,0:T(8,128)(2,1)S(1)}, u32[]{:S(2)}, u32[]{:S(2)}) collective-permute-start(bf16[64,1024]{1,0:T(8,128)(2,1)S(1)} %bitcast.46), channel_id=1, source_target_pairs={{0,0},{1,4},{2,8},{3,12},{16,16},{17,20},{24,24},{25,28},{4,1},{5,... | collective-permute-start | bytes 393224 | tf_op jit(solution)/shard_map/ppermute | solution.py:479
  66.6 7.2 %collective-permute-start.22 = (bf16[32,1024]{1,0:T(8,128)(2,1)S(1)}, bf16[32,1024]{1,0:T(8,128)(2,1)S(1)}, u32[]{:S(2)}, u32[]{:S(2)}) collective-permute-start(bf16[32,1024]{1,0:T(8,128)(2,1)S(1)} %bitcast.47), channel_id=1, source_target_pairs={{0,0},{1,4},{2,8},{3,12},{4,16},{5,20},{6,24},{7,28},{8,1},{9,5},{... | collective-permute-start | bytes 196616 | tf_op jit(solution)/shard_map/ppermute | solution.py:480
  68.6 6.9 %collective-permute-start.18 = (bf16[112,1024]{1,0:T(8,128)(2,1)S(1)}, bf16[112,1024]{1,0:T(8,128)(2,1)S(1)}, u32[]{:S(2)}, u32[]{:S(2)}) collective-permute-start(bf16[112,1024]{1,0:T(8,128)(2,1)S(1)} %collective-permute-done.17.refs_7_), channel_id=1, source_target_pairs={{0,4},{4,8},{8,12},{12,16},{16,20},{20,24},{24,28},{28,0},{1,5},{5... | collective-permute-start | bytes 688136 | tf_op jit(solution)/shard_map/ppermute | solution.py:31
  72.1 11.0 %collective-permute-start.20 = (bf16[64,1024]{1,0:T(8,128)(2,1)S(1)}, bf16[64,1024]{1,0:T(8,128)(2,1)S(1)}, u32[]{:S(2)}, u32[]{:S(2)}) collective-permute-start(bf16[64,1024]{1,0:T(8,128)(2,1)S(1)} %slice.56), channel_id=1, source_target_pairs={{0,28},{4,0},{8,4},{12,8},{16,12},{20,16},{24,20},{28,24},{1,29},{... | collective-permute-start | bytes 393224 | tf_op jit(solution)/shard_map/ppermute | solution.py:31
  75.4 7.6 %collective-permute-start.19 = (bf16[48,1024]{1,0:T(8,128)(2,1)S(1)}, bf16[48,1024]{1,0:T(8,128)(2,1)S(1)}, u32[]{:S(2)}, u32[]{:S(2)}) collective-permute-start(bf16[48,1024]{1,0:T(8,128)(2,1)S(1)} %slice.55), channel_id=1, source_target_pairs={{0,4},{4,8},{8,12},{12,16},{16,20},{20,24},{24,28},{28,0},{1,5},{5... | collective-permute-start | bytes 294920 | tf_op jit(solution)/shard_map/ppermute | solution.py:31
  90.2 2.3 %collective-permute-start.23 = (bf16[2,128,1152]{2,1,0:T(8,128)(2,1)}, bf16[2,128,1152]{2,1,0:T(8,128)(2,1)S(1)}, u32[]{:S(2)}, u32[]{:S(2)}) collective-permute-start(bf16[2,128,1152]{2,1,0:T(8,128)(2,1)} %get-tuple-element.185), channel_id=1, source_target_pairs={{0,1},{1,0},{2,3},{3,2},{4,5},{5,4},{6,7},{7,6},{8,9},{9,8},{10,11... | collective-permute-start | bytes 1769480 | tf_op jit(solution)/shard_map/ppermute | solution.py:31
  93.9 16.4 %collective-permute-start.24 = (bf16[2,128,1152]{2,1,0:T(8,128)(2,1)S(1)}, bf16[2,128,1152]{2,1,0:T(8,128)(2,1)S(1)}, u32[]{:S(2)}, u32[]{:S(2)}) collective-permute-start(bf16[2,128,1152]{2,1,0:T(8,128)(2,1)S(1)} %add_convert_fusion.near_ref), channel_id=1, source_target_pairs={{0,2},{2,0},{1,3},{3,1},{4,6},{6,4},{5,7},{7,5},{8,10},{10,8},{9,1... | collective-permute-start | bytes 1769480 | tf_op jit(solution)/shard_map/ppermute | solution.py:31
  97.0 7.0 %collective-permute-start.25 = (bf16[96,1024]{1,0:T(8,128)(2,1)S(1)}, bf16[96,1024]{1,0:T(8,128)(2,1)S(1)}, u32[]{:S(2)}, u32[]{:S(2)}) collective-permute-start(bf16[96,1024]{1,0:T(8,128)(2,1)S(1)} %pad_maximum_fusion.refs_0_.refs_1_), channel_id=1, source_target_pairs={{0,4},{4,8},{8,12},{12,16},{16,20},{20,24},{24,28},{28,0},{1,5},{5... | collective-permute-start | bytes 589832 | tf_op jit(solution)/shard_map/ppermute | solution.py:31
  98.6 5.5 %collective-permute-start.26 = (bf16[96,1024]{1,0:T(8,128)(2,1)S(1)}, bf16[96,1024]{1,0:T(8,128)(2,1)S(1)}, u32[]{:S(2)}, u32[]{:S(2)}) collective-permute-start(bf16[96,1024]{1,0:T(8,128)(2,1)S(1)} %pad_maximum_fusion.refs_0_.refs_1_), channel_id=1, source_target_pairs={{0,28},{4,0},{8,4},{12,8},{16,12},{20,16},{24,20},{28,24},{1,29},{... | collective-permute-start | bytes 589832 | tf_op jit(solution)/shard_map/ppermute | solution.py:31
  104.0 25.3 %copy-start.20 = (bf16[96,1024]{1,0:T(8,128)(2,1)}, bf16[96,1024]{1,0:T(8,128)(2,1)S(1)}, u32[]{:S(2)}) copy-start(bf16[96,1024]{1,0:T(8,128)(2,1)S(1)} %collective-permute-done.25.refs_7_.refs_8_) | copy-start | bytes 589828
  104.1 25.2 %copy-start.21 = (bf16[96,1024]{1,0:T(8,128)(2,1)}, bf16[96,1024]{1,0:T(8,128)(2,1)S(1)}, u32[]{:S(2)}) copy-start(bf16[96,1024]{1,0:T(8,128)(2,1)S(1)} %collective-permute-done.26.refs_1_.refs_2_) | copy-start | bytes 589828
  104.1 10.6 %collective-permute-start.27 = (bf16[96,1024]{1,0:T(8,128)(2,1)S(1)}, bf16[96,1024]{1,0:T(8,128)(2,1)S(1)}, u32[]{:S(2)}, u32[]{:S(2)}) collective-permute-start(bf16[96,1024]{1,0:T(8,128)(2,1)S(1)} %collective-permute-done.25.refs_7_.refs_8_), channel_id=1, source_target_pairs={{0,4},{4,8},{8,12},{12,16},{16,20},{20,24},{24,28},{28,0},{1,5},{5... | collective-permute-start | bytes 589832 | tf_op jit(solution)/shard_map/ppermute | solution.py:31
  105.5 9.2 %collective-permute-start.28 = (bf16[96,1024]{1,0:T(8,128)(2,1)S(1)}, bf16[96,1024]{1,0:T(8,128)(2,1)S(1)}, u32[]{:S(2)}, u32[]{:S(2)}) collective-permute-start(bf16[96,1024]{1,0:T(8,128)(2,1)S(1)} %collective-permute-done.26.refs_1_.refs_2_), channel_id=1, source_target_pairs={{0,28},{4,0},{8,4},{12,8},{16,12},{20,16},{24,20},{28,24},{1,29},{... | collective-permute-start | bytes 589832 | tf_op jit(solution)/shard_map/ppermute | solution.py:31
  113.8 15.5 %collective-permute-start.32 = (bf16[2,128,1024]{2,1,0:T(8,128)(2,1)}, bf16[2,128,1024]{2,1,0:T(8,128)(2,1)S(1)}, u32[]{:S(2)}, u32[]{:S(2)}) collective-permute-start(bf16[2,128,1024]{2,1,0:T(8,128)(2,1)} %get-tuple-element.193.refs_8_), channel_id=1, source_target_pairs={{0,1},{1,0},{2,3},{3,2},{4,5},{5,4},{6,7},{7,6},{8,9},{9,8},{10,11... | collective-permute-start | bytes 1572872 | tf_op jit(solution)/shard_map/ppermute | solution.py:31
  114.8 7.7 %collective-permute-start.30 = (bf16[96,1024]{1,0:T(8,128)(2,1)S(1)}, bf16[96,1024]{1,0:T(8,128)(2,1)S(1)}, u32[]{:S(2)}, u32[]{:S(2)}) collective-permute-start(bf16[96,1024]{1,0:T(8,128)(2,1)S(1)} %collective-permute-done.27.refs_6_.refs_7_), channel_id=1, source_target_pairs={{0,4},{4,8},{8,12},{12,16},{16,20},{20,24},{24,28},{28,0},{1,5},{5... | collective-permute-start | bytes 589832 | tf_op jit(solution)/shard_map/ppermute | solution.py:31
  116.5 6.4 %collective-permute-start.29 = (bf16[96,1024]{1,0:T(8,128)(2,1)S(1)}, bf16[96,1024]{1,0:T(8,128)(2,1)S(1)}, u32[]{:S(2)}, u32[]{:S(2)}) collective-permute-start(bf16[96,1024]{1,0:T(8,128)(2,1)S(1)} %collective-permute-done.28.refs_2_.refs_3_), channel_id=1, source_target_pairs={{0,28},{4,0},{8,4},{12,8},{16,12},{20,16},{24,20},{28,24},{1,29},{... | collective-permute-start | bytes 589832 | tf_op jit(solution)/shard_map/ppermute | solution.py:31
  122.5 6.8 %collective-permute-start.31 = (bf16[96,1024]{1,0:T(8,128)(2,1)S(1)}, bf16[96,1024]{1,0:T(8,128)(2,1)S(1)}, u32[]{:S(2)}, u32[]{:S(2)}) collective-permute-start(bf16[96,1024]{1,0:T(8,128)(2,1)S(1)} %collective-permute-done.30.refs_5_.refs_6_), channel_id=1, source_target_pairs={{0,4},{4,8},{8,12},{12,16},{16,20},{20,24},{24,28},{28,0},{1,5},{5... | collective-permute-start | bytes 589832 | tf_op jit(solution)/shard_map/ppermute | solution.py:31
  135.8 7.4 %collective-permute-start = (bf16[512,256]{1,0:T(8,128)(2,1)S(1)}, bf16[512,256]{1,0:T(8,128)(2,1)S(1)}, u32[]{:S(2)}, u32[]{:S(2)}) collective-permute-start(bf16[512,256]{1,0:T(8,128)(2,1)S(1)} %copy.27.up_ref), channel_id=1, source_target_pairs={{0,4},{4,8},{8,12},{12,16},{16,20},{20,24},{24,28},{28,0},{1,5},{5... | collective-permute-start | bytes 786440 | tf_op jit(solution)/shard_map/while/body/eval_jaxpr/ppermute | solution.py:31
  135.9 7.3 %collective-permute-start.1 = (bf16[512,256]{1,0:T(8,128)(2,1)S(1)}, bf16[512,256]{1,0:T(8,128)(2,1)S(1)}, u32[]{:S(2)}, u32[]{:S(2)}) collective-permute-start(bf16[512,256]{1,0:T(8,128)(2,1)S(1)} %copy.28.down_ref), channel_id=1, source_target_pairs={{0,28},{4,0},{8,4},{12,8},{16,12},{20,16},{24,20},{28,24},{1,29},{... | collective-permute-start | bytes 786440 | tf_op jit(solution)/shard_map/while/body/eval_jaxpr/ppermute | solution.py:31
  143.3 6.5 %collective-permute-start = (bf16[512,256]{1,0:T(8,128)(2,1)S(1)}, bf16[512,256]{1,0:T(8,128)(2,1)S(1)}, u32[]{:S(2)}, u32[]{:S(2)}) collective-permute-start(bf16[512,256]{1,0:T(8,128)(2,1)S(1)} %copy.27.up_ref), channel_id=1, source_target_pairs={{0,4},{4,8},{8,12},{12,16},{16,20},{20,24},{24,28},{28,0},{1,5},{5... | collective-permute-start | bytes 786440 | tf_op jit(solution)/shard_map/while/body/eval_jaxpr/ppermute | solution.py:31
  143.7 6.7 %collective-permute-start.1 = (bf16[512,256]{1,0:T(8,128)(2,1)S(1)}, bf16[512,256]{1,0:T(8,128)(2,1)S(1)}, u32[]{:S(2)}, u32[]{:S(2)}) collective-permute-start(bf16[512,256]{1,0:T(8,128)(2,1)S(1)} %copy.28.down_ref), channel_id=1, source_target_pairs={{0,28},{4,0},{8,4},{12,8},{16,12},{20,16},{24,20},{28,24},{1,29},{... | collective-permute-start | bytes 786440 | tf_op jit(solution)/shard_map/while/body/eval_jaxpr/ppermute | solution.py:31
  150.4 6.5 %collective-permute-start = (bf16[512,256]{1,0:T(8,128)(2,1)S(1)}, bf16[512,256]{1,0:T(8,128)(2,1)S(1)}, u32[]{:S(2)}, u32[]{:S(2)}) collective-permute-start(bf16[512,256]{1,0:T(8,128)(2,1)S(1)} %copy.27.up_ref), channel_id=1, source_target_pairs={{0,4},{4,8},{8,12},{12,16},{16,20},{20,24},{24,28},{28,0},{1,5},{5... | collective-permute-start | bytes 786440 | tf_op jit(solution)/shard_map/while/body/eval_jaxpr/ppermute | solution.py:31
  152.6 5.9 %collective-permute-start.1 = (bf16[512,256]{1,0:T(8,128)(2,1)S(1)}, bf16[512,256]{1,0:T(8,128)(2,1)S(1)}, u32[]{:S(2)}, u32[]{:S(2)}) collective-permute-start(bf16[512,256]{1,0:T(8,128)(2,1)S(1)} %copy.28.down_ref), channel_id=1, source_target_pairs={{0,28},{4,0},{8,4},{12,8},{16,12},{20,16},{24,20},{28,24},{1,29},{... | collective-permute-start | bytes 786440 | tf_op jit(solution)/shard_map/while/body/eval_jaxpr/ppermute | solution.py:31
  158.6 6.5 %collective-permute-start = (bf16[512,256]{1,0:T(8,128)(2,1)S(1)}, bf16[512,256]{1,0:T(8,128)(2,1)S(1)}, u32[]{:S(2)}, u32[]{:S(2)}) collective-permute-start(bf16[512,256]{1,0:T(8,128)(2,1)S(1)} %copy.27.up_ref), channel_id=1, source_target_pairs={{0,4},{4,8},{8,12},{12,16},{16,20},{20,24},{24,28},{28,0},{1,5},{5... | collective-permute-start | bytes 786440 | tf_op jit(solution)/shard_map/while/body/eval_jaxpr/ppermute | solution.py:31
  160.1 5.4 %collective-permute-start.1 = (bf16[512,256]{1,0:T(8,128)(2,1)S(1)}, bf16[512,256]{1,0:T(8,128)(2,1)S(1)}, u32[]{:S(2)}, u32[]{:S(2)}) collective-permute-start(bf16[512,256]{1,0:T(8,128)(2,1)S(1)} %copy.28.down_ref), channel_id=1, source_target_pairs={{0,28},{4,0},{8,4},{12,8},{16,12},{20,16},{24,20},{28,24},{1,29},{... | collective-permute-start | bytes 786440 | tf_op jit(solution)/shard_map/while/body/eval_jaxpr/ppermute | solution.py:31
  169.4 9.1 %collective-permute-start.33 = (bf16[2,128,1024]{2,1,0:T(8,128)(2,1)}, bf16[2,128,1024]{2,1,0:T(8,128)(2,1)S(1)}, u32[]{:S(2)}, u32[]{:S(2)}) collective-permute-start(bf16[2,128,1024]{2,1,0:T(8,128)(2,1)} %get-tuple-element.201), channel_id=1, source_target_pairs={{0,1},{1,0},{2,3},{3,2},{4,5},{5,4},{6,7},{7,6},{8,9},{9,8},{10,11... | collective-permute-start | bytes 1572872 | tf_op jit(solution)/shard_map/ppermute | solution.py:31
  178.8 11.2 %collective-permute-start.34 = (bf16[128,1024]{1,0:T(8,128)(2,1)S(1)}, bf16[128,1024]{1,0:T(8,128)(2,1)S(1)}, u32[]{:S(2)}, u32[]{:S(2)}) collective-permute-start(bf16[128,1024]{1,0:T(8,128)(2,1)S(1)} %fusion.3), channel_id=1, source_target_pairs={{0,32},{1,33},{2,34},{3,35},{32,64},{33,65},{34,66},{35,67},{64,96... | collective-permute-start | bytes 786440 | tf_op jit(solution)/shard_map/ppermute | solution.py:549
  179.6 16.7 %collective-permute-start.35 = (bf16[128,1024]{1,0:T(8,128)(2,1)S(1)}, bf16[128,1024]{1,0:T(8,128)(2,1)S(1)}, u32[]{:S(2)}, u32[]{:S(2)}) collective-permute-start(bf16[128,1024]{1,0:T(8,128)(2,1)S(1)} %fusion.6), channel_id=1, source_target_pairs={{0,34},{1,35},{2,32},{3,33},{32,66},{33,67},{34,64},{35,65},{64,98... | collective-permute-start | bytes 786440 | tf_op jit(solution)/shard_map/ppermute | solution.py:550
  (42 other events, 332.8 us)

commit v2 on v1

--- a/solution.py
+++ b/solution.py
@@ -337,11 +337,11 @@
 
 
 def project_kernel(at_ref, *refs):
-    packs = refs[0:8]
-    mine_ref, theirs_ref = refs[8:10]
-    q_ref, pack_ref = refs[10:12]
-    w_scr, h_scr, sems = refs[12:]
-    copies = fetch(views(packs, 0, 64), placed(at_ref, w_scr, 64), sems)
+    packs = refs[0:9]
+    mine_ref, theirs_ref = refs[9:11]
+    q_ref, pack_ref = refs[11:13]
+    w_scr, h_scr, sems = refs[13:]
+    copies = fetch(views(packs, 0, 64, 48), placed(at_ref, w_scr, 64), sems)
     x, c = at_ref[1], at_ref[2]
     for b, x_ in enumerate((x, 1 - x)):
         h_scr[rows_at(2 * x_ + c, ROWS), :] = mine_ref[b]
@@ -411,12 +411,12 @@
 
 
 def attend_kernel(at_ref, block_ref, *refs):
-    far_ref, weights = refs[0], refs[1:9]
-    q_ref, start_ref, acc_ref, stat_ref = refs[9:13]
-    keep_ref, send_ref = refs[13:15]
-    w_scr, c_scr, a_scr, s_scr, sems = refs[15:]
+    far_ref, weights = refs[0], refs[1:10]
+    q_ref, start_ref, acc_ref, stat_ref = refs[10:14]
+    keep_ref, send_ref = refs[14:16]
+    w_scr, c_scr, a_scr, s_scr, sems = refs[16:]
     z, first = at_ref[0], block_ref[0]
-    copies_w = fetch(views(weights, 64, 96), placed(at_ref, w_scr, 32), sems)
+    copies_w = fetch(views(weights, 64, 96, 48), placed(at_ref, w_scr, 32), sems)
     plane = z - PLANES // 2
     a_scr[...] = acc_ref[...]
     s_scr[...] = stat_ref[...]
@@ -475,9 +475,8 @@
     for j in range(4):
         mine = [4 * j, 4 * j + 1, 4 * j + 2, 4 * j + 3, 16 + 2 * j, 17 + 2 * j, 24 + 2 * j, 25 + 2 * j]
         qkv_slots += [(s, k * 4 + j) for k, s in enumerate(mine)]
-    turned, rows_out, _ = lax.optimization_barrier((jnp.transpose(w_qkv[0]), w_attn_out[0], weights))
-    turned = lax.ppermute(turned, CTX, qkv_slots)
-    rows_out = lax.ppermute(rows_out, CTX, order)
+    turned = lax.ppermute(jnp.transpose(w_qkv[0]), CTX, qkv_slots)
+    rows_out = lax.ppermute(w_attn_out[0], CTX, order)
     later = jnp.concatenate([turned, rows_out])
 
 
@@ -495,7 +494,6 @@
         space_kernel, [((TOKENS, 512), f32), ((TOKENS, LANES), f32)], [vmem] * 6,
         [pltpu.VMEM((STATE, 512), f32)], 1 << 30, 6 << 20,
         u, prm, head, skip, segc, segr)
-    y, later = lax.optimization_barrier((y, later))
     keep, send, start, first_block = local(
         leave_kernel,
         [((2, ROWS, MODEL + LANES), f32), ((2, ROWS, MODEL + LANES), bf16), ((TOKENS, LANES), jnp.int32),
@@ -505,9 +503,10 @@
          pltpu.VMEM((TOKENS, 512), bf16), pltpu.VMEM((TOKENS, LANES), f32), dma((16,))],
         1 << 30, 6 << 20,
         at, *packs, y, cum, prm, segc, gain_ssm)
-    near = (keep + swapped(send, "c").astype(f32)).astype(bf16)
+    near = swapped(send, "c")
+    near = (keep + near.astype(f32)).astype(bf16)
     far = swapped(near, "x")
-    weights = ring(later, None, (send, near, None))
+    weights = ring(later, 48, (None, near, None))
     hidden, first = local(
         hidden_kernel, [((2, ROWS, MODEL), bf16), ((ROWS, MODEL), f32)],
         [vmem] * 5, [], 1 << 20, 2 << 20,
@@ -515,8 +514,8 @@
 
     query, pack = local(
         project_kernel, [((TOKENS, 256), bf16), ((TOKENS, 256), bf16)],
-        [smem] + [whole] * 8 + [vmem] * 2,
-        [pltpu.VMEM((512, MODEL), bf16), pltpu.VMEM((TOKENS, MODEL), bf16), dma((8,))],
+        [smem] + [whole] * 9 + [vmem] * 2,
+        [pltpu.VMEM((512, MODEL), bf16), pltpu.VMEM((TOKENS, MODEL), bf16), dma((9,))],
         1 << 30, 4 << 20,
         at, *weights, hidden, swapped(hidden, "c"))
 
@@ -535,7 +534,7 @@
     far, _, acc, stat = lax.fori_loop(0, PLANES // 2, turn, (pack, pack, *empty))
     keep, send = local(
         attend_kernel, [((2, ROWS, MODEL), f32), ((2, ROWS, MODEL), bf16)],
-        [smem, smem, vmem] + [whole] * 8 + [vmem] * 4,
+        [smem, smem, vmem] + [whole] * 9 + [vmem] * 4,
         [pltpu.VMEM((256, MODEL), bf16), pltpu.VMEM((TOKENS, 256), bf16),
          pltpu.VMEM((TOKENS, 256), f32), pltpu.VMEM((TOKENS, LANES), f32), dma((8,))],
         1 << 30, 6 << 20,

time: 198 us -> 202 us (1.020)
  starting transfers between devices: 78.4 us -> 83.4 us
    ppermute x38 -> x39, starting transfers between devices: 66.6 us -> 75.4 us  [moved(): return lax.ppermute(value, axis, [(i, target(i)) for i in range(count)])]
    ppermute x2, starting transfers between devices: 10.9 us -> 5.55 us  [the longest x1 3.54 us: layer_pair(): rows_out = lax.ppermute(w_attn_out[0], CTX, order)]
    ppermute x2, waiting for transfers between devices: 1.04 us -> 6.35 us  [the longest x1 5.36 us: layer_pair(): rows_out = lax.ppermute(w_attn_out[0], CTX, order)]
    ppermute x38 -> x39, waiting for transfers between devices: 46.5 us -> 41.5 us  [moved(): return lax.ppermute(value, axis, [(i, target(i)) for i in range(count)])]
    ppermute x1, starting transfers between devices: 0.12 us -> 2.35 us  [layer_pair(): theirs = lax.ppermute(send, ('blk', 'x', 'c'), cross)]
    unnamed x82 -> x87, local copies, waits for them, and re-layouts: 5.85 us -> 5.9 us
  transfers between devices with their start and end apart: 42 -> 43, of which waited for: 23 -> 21; matrix products, arithmetic and copies ran while one was open for 4% -> 4% of each run, Pallas kernels for 9% -> 9%
where the time goes in v2:
time: 202 us; the launch traced here: 201 us
  starting transfers between devices  83.4 us (41%)
  waiting for transfers between devices  63 us (31%)
  Pallas kernels  39 us (19%)
  local copies, waits for them, and re-layouts  9.3 us (5%)
  other arithmetic  5.25 us (3%)
    ppermute x39, starting transfers between devices, moved(): return lax.ppermute(value, axis, [(i, target(i)) for i in range(count)])  75.4 us
    ppermute x39, waiting for transfers between devices, moved(): return lax.ppermute(value, axis, [(i, target(i)) for i in range(count)])  41.5 us
    pallas_call x10, Pallas kernels, local(): pl.pallas_call(kernel, out_shape=tuple((jax.ShapeDtypeStruct(shape, kind)...  39 us
    ppermute x1, waiting for transfers between devices, layer_pair(): mine = lax.ppermute(mine, ('blk', 'x', 'c'), straight)  8.79 us
    ppermute x1, waiting for transfers between devices, layer_pair(): theirs = lax.ppermute(send, ('blk', 'x', 'c'), cross)  6.33 us
    unnamed x87, local copies, waits for them, and re-layouts  5.9 us
    ppermute x1, waiting for transfers between devices, layer_pair(): rows_out = lax.ppermute(w_attn_out[0], CTX, order)  5.36 us
  transfers between devices with their start and end apart: 43, of which 21 were waited for; matrix products, arithmetic and copies ran while one was open for 4% of the time, Pallas kernels for 9%

profile of v2, /device:TPU:1, one launch (start us, length us, event | category | flops | bytes accessed | tf_op | source)
XLA Modules:
  0.0 201.2 jit_solution(9186926214752557873)
XLA Ops:
  0.0 6.4 %collective-permute-start.3 = (bf16[64,1024]{1,0:T(8,128)(2,1)}, bf16[64,1024]{1,0:T(8,128)(2,1)S(1)}, u32[]{:S(2)}, u32[]{:S(2)}) collective-permute-start(bf16[64,1024]{1,0:T(8,128)(2,1)} %bitcast.42), channel_id=1, source_target_pairs={{0,28},{4,0},{8,4},{12,8},{16,12},{20,16},{24,20},{28,24},{1,29},{... | collective-permute-start | bytes 393224 | tf_op jit(solution)/shard_map/ppermute | solution.py:31
  8.0 5.3 %collective-permute-start.2 = (bf16[144,1024]{1,0:T(8,128)(2,1)S(1)}, bf16[144,1024]{1,0:T(8,128)(2,1)S(1)}, u32[]{:S(2)}, u32[]{:S(2)}) collective-permute-start(bf16[144,1024]{1,0:T(8,128)(2,1)S(1)} %fusion.4), channel_id=1, source_target_pairs={{0,224},{32,0},{64,32},{96,64},{128,96},{160,128},{192,160},{224,1... | collective-permute-start | bytes 884744 | tf_op jit(solution)/shard_map/ppermute | solution.py:31
  15.0 2.7 %collective-permute-start.4 = (bf16[64,1024]{1,0:T(8,128)(2,1)S(1)}, bf16[64,1024]{1,0:T(8,128)(2,1)S(1)}, u32[]{:S(2)}, u32[]{:S(2)}) collective-permute-start(bf16[64,1024]{1,0:T(8,128)(2,1)S(1)} %collective-permute-done.3.refs_5_), channel_id=1, source_target_pairs={{0,28},{4,0},{8,4},{12,8},{16,12},{20,16},{24,20},{28,24},{1,29},{... | collective-permute-start | bytes 393224 | tf_op jit(solution)/shard_map/ppermute | solution.py:31
  17.9 1.8 collective-permute-done.4.refs_6_
  19.7 3.1 %collective-permute-done.6.refs_10_ = bf16[64,1024]{1,0:T(8,128)(2,1)S(1)} collective-permute-done((bf16[64,1024]{1,0:T(8,128)(2,1)S(1)}, bf16[64,1024]{1,0:T(8,128)(2,1)S(1)}, u32[]{:S(2)}, u32[]{:S(2)}) %collective-permute-start.6) | collective-permute-done | bytes 131104 | tf_op jit(solution)/shard_map/ppermute | solution.py:31
  24.9 2.7 %collective-permute-start.10 = (bf16[64,1024]{1,0:T(8,128)(2,1)S(1)}, bf16[64,1024]{1,0:T(8,128)(2,1)S(1)}, u32[]{:S(2)}, u32[]{:S(2)}) collective-permute-start(bf16[64,1024]{1,0:T(8,128)(2,1)S(1)} %collective-permute-done.4.refs_6_), channel_id=1, source_target_pairs={{0,28},{4,0},{8,4},{12,8},{16,12},{20,16},{24,20},{28,24},{1,29},{... | collective-permute-start | bytes 393224 | tf_op jit(solution)/shard_map/ppermute | solution.py:31
  27.6 3.8 %collective-permute-start.8 = (bf16[144,1024]{1,0:T(8,128)(2,1)S(1)}, bf16[144,1024]{1,0:T(8,128)(2,1)S(1)}, u32[]{:S(2)}, u32[]{:S(2)}) collective-permute-start(bf16[144,1024]{1,0:T(8,128)(2,1)S(1)} %collective-permute-done.2.refs_0_.own_ref), channel_id=1, source_target_pairs={{0,1},{1,0},{2,3},{3,2},{4,5},{5,4},{6,7},{7,6},{8,9},{9,8},{10,11... | collective-permute-start | bytes 884744 | tf_op jit(solution)/shard_map/ppermute | solution.py:31
  31.4 2.4 %collective-permute-start.9 = (bf16[144,1024]{1,0:T(8,128)(2,1)S(1)}, bf16[144,1024]{1,0:T(8,128)(2,1)S(1)}, u32[]{:S(2)}, u32[]{:S(2)}) collective-permute-start(bf16[144,1024]{1,0:T(8,128)(2,1)S(1)} %collective-permute-done.7.refs_1_.other_ref), channel_id=1, source_target_pairs={{0,1},{1,0},{2,3},{3,2},{4,5},{5,4},{6,7},{7,6},{8,9},{9,8},{10,11... | collective-permute-start | bytes 884744 | tf_op jit(solution)/shard_map/ppermute | solution.py:31
  37.2 6.0 %shard_map.118 = (bf16[512,512]{1,0:T(8,128)(2,1)}, f32[512,256]{1,0:T(8,128)}, f32[512,128]{1,0:T(8,128)}, f32[1,512]{1,0:T(1,128)}, bf16[112,1024]{1,0:T(8,128)(2,1)}) custom-call(s32[3]{0:T(128)S(1)} %pad_add_fusion.at_ref, bf16[144,1024]{1,0:T(8,128)(2,1)} %copy-done.6, bf16[144,1024]{1,0:T(8,128)(2,1)} %copy-done.7, bf16[144,1024]{1,0:T(8,128)(2,1)} %copy-done.16, ...), custom_call_target="tpu_custom_call" | custom-call | flops 1073741824 | bytes 6291456 | tf_op jit(solution)/shard_map/pallas_call | solution.py:66
  44.8 3.6 %collective-permute-done.13.refs_1_ = bf16[112,1024]{1,0:T(8,128)(2,1)S(1)} collective-permute-done((bf16[112,1024]{1,0:T(8,128)(2,1)}, bf16[112,1024]{1,0:T(8,128)(2,1)S(1)}, u32[]{:S(2)}, u32[]{:S(2)}) %collective-permute-start.13) | collective-permute-done | bytes 229408 | tf_op jit(solution)/shard_map/ppermute | solution.py:31
  48.4 2.9 %collective-permute-start.14 = (bf16[112,1024]{1,0:T(8,128)(2,1)S(1)}, bf16[112,1024]{1,0:T(8,128)(2,1)S(1)}, u32[]{:S(2)}, u32[]{:S(2)}) collective-permute-start(bf16[112,1024]{1,0:T(8,128)(2,1)S(1)} %collective-permute-done.13.refs_1_), channel_id=1, source_target_pairs={{0,28},{4,0},{8,4},{12,8},{16,12},{20,16},{24,20},{28,24},{1,29},{... | collective-permute-start | bytes 688136 | tf_op jit(solution)/shard_map/ppermute | solution.py:31
  51.4 3.4 %collective-permute-done.14.refs_2_ = bf16[112,1024]{1,0:T(8,128)(2,1)S(1)} collective-permute-done((bf16[112,1024]{1,0:T(8,128)(2,1)S(1)}, bf16[112,1024]{1,0:T(8,128)(2,1)S(1)}, u32[]{:S(2)}, u32[]{:S(2)}) %collective-permute-start.14) | collective-permute-done | bytes 229408 | tf_op jit(solution)/shard_map/ppermute | solution.py:31
  54.8 2.6 %collective-permute-start.15 = (bf16[112,1024]{1,0:T(8,128)(2,1)S(1)}, bf16[112,1024]{1,0:T(8,128)(2,1)S(1)}, u32[]{:S(2)}, u32[]{:S(2)}) collective-permute-start(bf16[112,1024]{1,0:T(8,128)(2,1)S(1)} %collective-permute-done.14.refs_2_), channel_id=1, source_target_pairs={{0,28},{4,0},{8,4},{12,8},{16,12},{20,16},{24,20},{28,24},{1,29},{... | collective-permute-start | bytes 688136 | tf_op jit(solution)/shard_map/ppermute | solution.py:31
  57.8 4.4 %collective-permute-done.15.refs_3_ = bf16[112,1024]{1,0:T(8,128)(2,1)S(1)} collective-permute-done((bf16[112,1024]{1,0:T(8,128)(2,1)S(1)}, bf16[112,1024]{1,0:T(8,128)(2,1)S(1)}, u32[]{:S(2)}, u32[]{:S(2)}) %collective-permute-start.15) | collective-permute-done | bytes 229408 | tf_op jit(solution)/shard_map/ppermute | solution.py:31
  65.3 6.1 %shard_map.119 = (f32[512,512]{1,0:T(8,128)}, f32[512,128]{1,0:T(8,128)}) custom-call(bf16[512,512]{1,0:T(8,128)(2,1)} %get-tuple-element.169.u_ref, f32[512,256]{1,0:T(8,128)} %get-tuple-element.170.prm_ref.refs_11_, f32[8,128]{1,0:T(8,128)} %pad.9.refs_15_.head_ref, f32[1,512]{1,0:T(1,128)} %broadcast_in_dim_reshape.3.skip_ref, ...), custom_call_target="tpu_custom_call" | custom-call | flops 1073741824 | bytes 6291456 | tf_op jit(solution)/shard_map/pallas_call | solution.py:66
  72.1 6.6 %shard_map.120 = (f32[2,128,1152]{2,1,0:T(8,128)}, bf16[2,128,1152]{2,1,0:T(8,128)(2,1)}, s32[512,128]{1,0:T(8,128)}, s32[1]{0:T(128)}) custom-call(s32[3]{0:T(128)S(1)} %pad_add_fusion.at_ref, bf16[112,1024]{1,0:T(8,128)(2,1)} %get-tuple-element.168.refs_0_, bf16[112,1024]{1,0:T(8,128)(2,1)} %copy-done.18, bf16[112,1024]{1,0:T(8,128)(2,1)} %copy-done.20, ...), custom_call_target="tpu_custom_call" | custom-call | flops 1073741824 | bytes 6291456 | tf_op jit(solution)/shard_map/pallas_call | solution.py:66
  78.7 7.9 %collective-permute-start.21 = (bf16[2,128,1152]{2,1,0:T(8,128)(2,1)}, bf16[2,128,1152]{2,1,0:T(8,128)(2,1)S(1)}, u32[]{:S(2)}, u32[]{:S(2)}) collective-permute-start(bf16[2,128,1152]{2,1,0:T(8,128)(2,1)} %get-tuple-element.176), channel_id=1, source_target_pairs={{0,1},{1,0},{2,3},{3,2},{4,5},{5,4},{6,7},{7,6},{8,9},{9,8},{10,11... | collective-permute-start | bytes 1769480 | tf_op jit(solution)/shard_map/ppermute | solution.py:31
  86.6 1.8 collective-permute-done.21
  91.1 2.0 %collective-permute-start.23 = (bf16[64,1024]{1,0:T(8,128)(2,1)S(1)}, bf16[64,1024]{1,0:T(8,128)(2,1)S(1)}, u32[]{:S(2)}, u32[]{:S(2)}) collective-permute-start(bf16[64,1024]{1,0:T(8,128)(2,1)S(1)} %bitcast.46), channel_id=1, source_target_pairs={{0,0},{1,4},{2,8},{3,12},{16,16},{17,20},{24,24},{25,28},{4,1},{5,... | collective-permute-start | bytes 393224 | tf_op jit(solution)/shard_map/ppermute | solution.py:478
  93.1 3.5 %collective-permute-start.24 = (bf16[32,1024]{1,0:T(8,128)(2,1)S(1)}, bf16[32,1024]{1,0:T(8,128)(2,1)S(1)}, u32[]{:S(2)}, u32[]{:S(2)}) collective-permute-start(bf16[32,1024]{1,0:T(8,128)(2,1)S(1)} %bitcast.47), channel_id=1, source_target_pairs={{0,0},{1,4},{2,8},{3,12},{4,16},{5,20},{6,24},{7,28},{8,1},{9,5},{... | collective-permute-start | bytes 196616 | tf_op jit(solution)/shard_map/ppermute | solution.py:479
  97.6 5.4 %collective-permute-done.24 = bf16[32,1024]{1,0:T(8,128)(2,1)S(1)} collective-permute-done((bf16[32,1024]{1,0:T(8,128)(2,1)S(1)}, bf16[32,1024]{1,0:T(8,128)(2,1)S(1)}, u32[]{:S(2)}, u32[]{:S(2)}) %collective-permute-start.24) | collective-permute-done | bytes 65568 | tf_op jit(solution)/shard_map/ppermute | solution.py:479
  103.1 5.7 %collective-permute-start.25 = (bf16[96,1024]{1,0:T(8,128)(2,1)S(1)}, bf16[96,1024]{1,0:T(8,128)(2,1)S(1)}, u32[]{:S(2)}, u32[]{:S(2)}) collective-permute-start(bf16[96,1024]{1,0:T(8,128)(2,1)S(1)} %constant_dynamic-update-slice_fusion.refs_0_.refs_1_), channel_id=1, source_target_pairs={{0,28},{4,0},{8,4},{12,8},{16,12},{20,16},{24,20},{28,24},{1,29},{... | collective-permute-start | bytes 589832 | tf_op jit(solution)/shard_map/ppermute | solution.py:31
  109.6 2.7 %shard_map.121 = (bf16[2,128,1024]{2,1,0:T(8,128)(2,1)}, f32[128,1024]{1,0:T(8,128)}) custom-call(bf16[144,1024]{1,0:T(8,128)(2,1)} %copy-done.6, bf16[144,1024]{1,0:T(8,128)(2,1)} %copy-done.7, bf16[2,128,1152]{2,1,0:T(8,128)(2,1)} %copy-done.2, bf16[2,128,1152]{2,1,0:T(8,128)(2,1)} %copy-done.4, bf16[1,1024]{1,0:T(2,128)(2,1)} %get-tuple-element.210.gain_ref), custom_call_target="tpu_custom_call" | custom-call | flops 1048576 | bytes 2097152 | tf_op jit(solution)/shard_map/pallas_call | solution.py:66
  112.5 2.7 %collective-permute-start.28 = (bf16[96,1024]{1,0:T(8,128)(2,1)S(1)}, bf16[96,1024]{1,0:T(8,128)(2,1)S(1)}, u32[]{:S(2)}, u32[]{:S(2)}) collective-permute-start(bf16[96,1024]{1,0:T(8,128)(2,1)S(1)} %collective-permute-done.25.refs_1_.refs_2_), channel_id=1, source_target_pairs={{0,28},{4,0},{8,4},{12,8},{16,12},{20,16},{24,20},{28,24},{1,29},{... | collective-permute-start | bytes 589832 | tf_op jit(solution)/shard_map/ppermute | solution.py:31
  115.2 4.4 %collective-permute-done.27.refs_7_.refs_8_ = bf16[96,1024]{1,0:T(8,128)(2,1)S(1)} collective-permute-done((bf16[96,1024]{1,0:T(8,128)(2,1)S(1)}, bf16[96,1024]{1,0:T(8,128)(2,1)S(1)}, u32[]{:S(2)}, u32[]{:S(2)}) %collective-permute-start.27) | collective-permute-done | bytes 196640 | tf_op jit(solution)/shard_map/ppermute | solution.py:31
  120.2 2.2 %collective-permute-start.29 = (bf16[96,1024]{1,0:T(8,128)(2,1)S(1)}, bf16[96,1024]{1,0:T(8,128)(2,1)S(1)}, u32[]{:S(2)}, u32[]{:S(2)}) collective-permute-start(bf16[96,1024]{1,0:T(8,128)(2,1)S(1)} %collective-permute-done.28.refs_2_.refs_3_), channel_id=1, source_target_pairs={{0,28},{4,0},{8,4},{12,8},{16,12},{20,16},{24,20},{28,24},{1,29},{... | collective-permute-start | bytes 589832 | tf_op jit(solution)/shard_map/ppermute | solution.py:31
  122.4 3.7 %collective-permute-done.30.refs_6_.refs_7_ = bf16[96,1024]{1,0:T(8,128)(2,1)S(1)} collective-permute-done((bf16[96,1024]{1,0:T(8,128)(2,1)S(1)}, bf16[96,1024]{1,0:T(8,128)(2,1)S(1)}, u32[]{:S(2)}, u32[]{:S(2)}) %collective-permute-start.30) | collective-permute-done | bytes 196640 | tf_op jit(solution)/shard_map/ppermute | solution.py:31
  126.3 2.7 %collective-permute-start.32 = (bf16[48,1024]{1,0:T(8,128)(2,1)S(1)}, bf16[48,1024]{1,0:T(8,128)(2,1)S(1)}, u32[]{:S(2)}, u32[]{:S(2)}) collective-permute-start(bf16[48,1024]{1,0:T(8,128)(2,1)S(1)} %slice.66), channel_id=1, source_target_pairs={{0,28},{4,0},{8,4},{12,8},{16,12},{20,16},{24,20},{28,24},{1,29},{... | collective-permute-start | bytes 294920 | tf_op jit(solution)/shard_map/ppermute | solution.py:31
  129.0 1.9 collective-permute-done.31.refs_4_.refs_5_
  132.4 4.0 %shard_map.122 = (bf16[512,256]{1,0:T(8,128)(2,1)}, bf16[512,256]{1,0:T(8,128)(2,1)S(1)}) custom-call(s32[3]{0:T(128)S(1)} %pad_add_fusion.at_ref, bf16[96,1024]{1,0:T(8,128)(2,1)} %copy-done.8, bf16[96,1024]{1,0:T(8,128)(2,1)} %copy-done.23, bf16[96,1024]{1,0:T(8,128)(2,1)} %copy-done.25, bf16[96,1024]{1,0:T(8,128)(2,1)} %copy-done.11, ...), custom_call_target="tpu_custom_call" | custom-call | flops 1073741824 | bytes 4194304 | tf_op jit(solution)/shard_map/pallas_call | solution.py:66
  137.5 31.3 %while.19 = (s32[]{:T(128)}, bf16[512,256]{1,0:T(8,128)(2,1)S(1)}, bf16[512,256]{1,0:T(8,128)(2,1)S(1)}, f32[512,256]{1,0:T(8,128)S(1)}, f32[512,128]{1,0:T(8,12...) while((s32[]{:T(128)}, bf16[512,256]{1,0:T(8,128)(2,1)S(1)}, ...), condition=%wide.region_1.2_spmd, body=%wide.region_0.1_spmd.sunk | while | flops 1073741824 | bytes 8388853 | solution.py:534
  138.2 2.2 %collective-permute-start.1 = (bf16[512,256]{1,0:T(8,128)(2,1)S(1)}, bf16[512,256]{1,0:T(8,128)(2,1)S(1)}, u32[]{:S(2)}, u32[]{:S(2)}) collective-permute-start(bf16[512,256]{1,0:T(8,128)(2,1)S(1)} %copy.29.down_ref), channel_id=1, source_target_pairs={{0,28},{4,0},{8,4},{12,8},{16,12},{20,16},{24,20},{28,24},{1,29},{... | collective-permute-start | bytes 786440 | tf_op jit(solution)/shard_map/while/body/eval_jaxpr/ppermute | solution.py:31
  140.4 4.1 %eval_jaxpr.5 = (f32[512,256]{1,0:T(8,128)S(1)}, f32[512,128]{1,0:T(8,128)S(1)}) custom-call(s32[3]{0:T(128)S(1)} %get-tuple-element.296.at_ref, s32[1]{0:T(128)} %get-tuple-element.297.block_ref, s32[1]{0:T(128)} %bitcast.37.r_ref, bf16[512,256]{1,0:T(8,128)(2,1)} %copy-done, ...), custom_call_target="tpu_custom_call", output_to_operand_aliasing={{0}: (7, {}), {1}: (8, {})} | custom-call | flops 1073741824 | bytes 3145728 | tf_op jit(solution)/shard_map/while/body/eval_jaxpr/pallas_call | solution.py:66
  144.6 1.8 collective-permute-start
  147.5 1.9 eval_jaxpr.5
  151.7 1.8 collective-permute-start
  154.6 1.9 eval_jaxpr.5
  156.5 1.9 collective-permute-done
  159.1 1.8 collective-permute-start
  162.0 1.9 eval_jaxpr.5
  163.9 3.0 %collective-permute-done = bf16[512,256]{1,0:T(8,128)(2,1)S(1)} collective-permute-done((bf16[512,256]{1,0:T(8,128)(2,1)S(1)}, bf16[512,256]{1,0:T(8,128)(2,1)S(1)}, u32[]{:S(2)}, u32[]{:S(2)}) %collective-permute-start) | collective-permute-done | bytes 262176 | tf_op jit(solution)/shard_map/while/body/eval_jaxpr/ppermute | solution.py:31
  166.9 1.8 collective-permute-done.1
  168.8 3.8 %shard_map.123 = (f32[2,128,1024]{2,1,0:T(8,128)}, bf16[2,128,1024]{2,1,0:T(8,128)(2,1)}) custom-call(s32[3]{0:T(128)S(1)} %get-tuple-element.331, s32[1]{0:T(128)} %get-tuple-element.277.block_ref, bf16[512,256]{1,0:T(8,128)(2,1)S(1)} %get-tuple-element.185.refs_0_, bf16[96,1024]{1,0:T(8,128)(2,1)} %copy-done.8, bf16[96,1024]{1,0:T(8,128)(2,1)} %copy-done.23, ...), custom_call_target="tpu_custom_call" | custom-call | flops 1073741824 | bytes 6291456 | tf_op jit(solution)/shard_map/pallas_call | solution.py:66
  172.6 8.2 %collective-permute-start.34 = (bf16[2,128,1024]{2,1,0:T(8,128)(2,1)}, bf16[2,128,1024]{2,1,0:T(8,128)(2,1)S(1)}, u32[]{:S(2)}, u32[]{:S(2)}) collective-permute-start(bf16[2,128,1024]{2,1,0:T(8,128)(2,1)} %get-tuple-element.189), channel_id=1, source_target_pairs={{0,1},{1,0},{2,3},{3,2},{4,5},{5,4},{6,7},{7,6},{8,9},{9,8},{10,11... | collective-permute-start | bytes 1572872 | tf_op jit(solution)/shard_map/ppermute | solution.py:31
  180.8 1.7 collective-permute-done.34
  183.0 2.3 %collective-permute-start.36 = (bf16[128,1024]{1,0:T(8,128)(2,1)S(1)}, bf16[128,1024]{1,0:T(8,128)(2,1)S(1)}, u32[]{:S(2)}, u32[]{:S(2)}) collective-permute-start(bf16[128,1024]{1,0:T(8,128)(2,1)S(1)} %fusion.6), channel_id=1, source_target_pairs={{0,34},{1,35},{2,32},{3,33},{32,66},{33,67},{34,64},{35,65},{64,98... | collective-permute-start | bytes 786440 | tf_op jit(solution)/shard_map/ppermute | solution.py:549
  185.3 8.8 %collective-permute-done.35 = bf16[128,1024]{1,0:T(8,128)(2,1)S(1)} collective-permute-done((bf16[128,1024]{1,0:T(8,128)(2,1)S(1)}, bf16[128,1024]{1,0:T(8,128)(2,1)S(1)}, u32[]{:S(2)}, u32[]{:S(2)}) %collective-permute-start.35) | collective-permute-done | bytes 262176 | tf_op jit(solution)/shard_map/ppermute | solution.py:548
  194.1 6.3 %collective-permute-done.36 = bf16[128,1024]{1,0:T(8,128)(2,1)S(1)} collective-permute-done((bf16[128,1024]{1,0:T(8,128)(2,1)S(1)}, bf16[128,1024]{1,0:T(8,128)(2,1)S(1)}, u32[]{:S(2)}, u32[]{:S(2)}) %collective-permute-start.36) | collective-permute-done | bytes 262176 | tf_op jit(solution)/shard_map/ppermute | solution.py:549
  (193 shorter events, 30.5 us)
Async XLA Ops:
  0.0 15.0 %collective-permute-start.3 = (bf16[64,1024]{1,0:T(8,128)(2,1)}, bf16[64,1024]{1,0:T(8,128)(2,1)S(1)}, u32[]{:S(2)}, u32[]{:S(2)}) collective-permute-start(bf16[64,1024]{1,0:T(8,128)(2,1)} %bitcast.42), channel_id=1, source_target_pairs={{0,28},{4,0},{8,4},{12,8},{16,12},{20,16},{24,20},{28,24},{1,29},{... | collective-permute-start | bytes 393224 | tf_op jit(solution)/shard_map/ppermute | solution.py:31
  6.4 11.4 %collective-permute-start.5 = (bf16[64,1024]{1,0:T(8,128)(2,1)}, bf16[64,1024]{1,0:T(8,128)(2,1)S(1)}, u32[]{:S(2)}, u32[]{:S(2)}) collective-permute-start(bf16[64,1024]{1,0:T(8,128)(2,1)} %bitcast.43), channel_id=1, source_target_pairs={{0,4},{4,8},{8,12},{12,16},{16,20},{20,24},{24,28},{28,0},{1,5},{5... | collective-permute-start | bytes 393224 | tf_op jit(solution)/shard_map/ppermute | solution.py:31
  8.0 14.8 %collective-permute-start.2 = (bf16[144,1024]{1,0:T(8,128)(2,1)S(1)}, bf16[144,1024]{1,0:T(8,128)(2,1)S(1)}, u32[]{:S(2)}, u32[]{:S(2)}) collective-permute-start(bf16[144,1024]{1,0:T(8,128)(2,1)S(1)} %fusion.4), channel_id=1, source_target_pairs={{0,224},{32,0},{64,32},{96,64},{128,96},{160,128},{192,160},{224,1... | collective-permute-start | bytes 884744 | tf_op jit(solution)/shard_map/ppermute | solution.py:31
  15.0 4.7 %collective-permute-start.4 = (bf16[64,1024]{1,0:T(8,128)(2,1)S(1)}, bf16[64,1024]{1,0:T(8,128)(2,1)S(1)}, u32[]{:S(2)}, u32[]{:S(2)}) collective-permute-start(bf16[64,1024]{1,0:T(8,128)(2,1)S(1)} %collective-permute-done.3.refs_5_), channel_id=1, source_target_pairs={{0,28},{4,0},{8,4},{12,8},{16,12},{20,16},{24,20},{28,24},{1,29},{... | collective-permute-start | bytes 393224 | tf_op jit(solution)/shard_map/ppermute | solution.py:31
  17.8 5.0 %collective-permute-start.6 = (bf16[64,1024]{1,0:T(8,128)(2,1)S(1)}, bf16[64,1024]{1,0:T(8,128)(2,1)S(1)}, u32[]{:S(2)}, u32[]{:S(2)}) collective-permute-start(bf16[64,1024]{1,0:T(8,128)(2,1)S(1)} %collective-permute-done.5.refs_11_), channel_id=1, source_target_pairs={{0,4},{4,8},{8,12},{12,16},{16,20},{20,24},{24,28},{28,0},{1,5},{5... | collective-permute-start | bytes 393224 | tf_op jit(solution)/shard_map/ppermute | solution.py:31
  22.8 8.6 %collective-permute-start.7 = (bf16[144,1024]{1,0:T(8,128)(2,1)S(1)}, bf16[144,1024]{1,0:T(8,128)(2,1)S(1)}, u32[]{:S(2)}, u32[]{:S(2)}) collective-permute-start(bf16[144,1024]{1,0:T(8,128)(2,1)S(1)} %collective-permute-done.2.refs_0_.own_ref), channel_id=1, source_target_pairs={{0,2},{2,0},{1,3},{3,1},{4,6},{6,4},{5,7},{7,5},{8,10},{10,8},{9,1... | collective-permute-start | bytes 884744 | tf_op jit(solution)/shard_map/ppermute | solution.py:31
  24.3 7.1 %collective-permute-start.11 = (bf16[64,1024]{1,0:T(8,128)(2,1)S(1)}, bf16[64,1024]{1,0:T(8,128)(2,1)S(1)}, u32[]{:S(2)}, u32[]{:S(2)}) collective-permute-start(bf16[64,1024]{1,0:T(8,128)(2,1)S(1)} %collective-permute-done.6.refs_10_), channel_id=1, source_target_pairs={{0,4},{4,8},{8,12},{12,16},{16,20},{20,24},{24,28},{28,0},{1,5},{5... | collective-permute-start | bytes 393224 | tf_op jit(solution)/shard_map/ppermute | solution.py:31
  24.9 9.8 %collective-permute-start.10 = (bf16[64,1024]{1,0:T(8,128)(2,1)S(1)}, bf16[64,1024]{1,0:T(8,128)(2,1)S(1)}, u32[]{:S(2)}, u32[]{:S(2)}) collective-permute-start(bf16[64,1024]{1,0:T(8,128)(2,1)S(1)} %collective-permute-done.4.refs_6_), channel_id=1, source_target_pairs={{0,28},{4,0},{8,4},{12,8},{16,12},{20,16},{24,20},{28,24},{1,29},{... | collective-permute-start | bytes 393224 | tf_op jit(solution)/shard_map/ppermute | solution.py:31
  27.6 8.8 %collective-permute-start.8 = (bf16[144,1024]{1,0:T(8,128)(2,1)S(1)}, bf16[144,1024]{1,0:T(8,128)(2,1)S(1)}, u32[]{:S(2)}, u32[]{:S(2)}) collective-permute-start(bf16[144,1024]{1,0:T(8,128)(2,1)S(1)} %collective-permute-done.2.refs_0_.own_ref), channel_id=1, source_target_pairs={{0,1},{1,0},{2,3},{3,2},{4,5},{5,4},{6,7},{7,6},{8,9},{9,8},{10,11... | collective-permute-start | bytes 884744 | tf_op jit(solution)/shard_map/ppermute | solution.py:31
  31.4 5.0 %collective-permute-start.12 = (bf16[64,1024]{1,0:T(8,128)(2,1)S(1)}, bf16[64,1024]{1,0:T(8,128)(2,1)S(1)}, u32[]{:S(2)}, u32[]{:S(2)}) collective-permute-start(bf16[64,1024]{1,0:T(8,128)(2,1)S(1)} %collective-permute-done.11.refs_9_), channel_id=1, source_target_pairs={{0,4},{4,8},{8,12},{12,16},{16,20},{20,24},{24,28},{28,0},{1,5},{5... | collective-permute-start | bytes 393224 | tf_op jit(solution)/shard_map/ppermute | solution.py:31
  31.4 5.0 %collective-permute-start.9 = (bf16[144,1024]{1,0:T(8,128)(2,1)S(1)}, bf16[144,1024]{1,0:T(8,128)(2,1)S(1)}, u32[]{:S(2)}, u32[]{:S(2)}) collective-permute-start(bf16[144,1024]{1,0:T(8,128)(2,1)S(1)} %collective-permute-done.7.refs_1_.other_ref), channel_id=1, source_target_pairs={{0,1},{1,0},{2,3},{3,2},{4,5},{5,4},{6,7},{7,6},{8,9},{9,8},{10,11... | collective-permute-start | bytes 884744 | tf_op jit(solution)/shard_map/ppermute | solution.py:31
  37.2 20.2 %copy-start.14 = (bf16[1,2048]{1,0:T(2,128)(2,1)S(1)}, bf16[1,2048]{1,0:T(2,128)(2,1)}, u32[]{:S(2)}) copy-start(bf16[1,2048]{1,0:T(2,128)(2,1)} %param.22) | copy-start | bytes 12292
  43.3 5.2 %collective-permute-start.13 = (bf16[112,1024]{1,0:T(8,128)(2,1)}, bf16[112,1024]{1,0:T(8,128)(2,1)S(1)}, u32[]{:S(2)}, u32[]{:S(2)}) collective-permute-start(bf16[112,1024]{1,0:T(8,128)(2,1)} %get-tuple-element.168.refs_0_), channel_id=1, source_target_pairs={{0,28},{4,0},{8,4},{12,8},{16,12},{20,16},{24,20},{28,24},{1,29},{... | collective-permute-start | bytes 688136 | tf_op jit(solution)/shard_map/ppermute | solution.py:31
  44.6 6.7 %collective-permute-start.16 = (bf16[112,1024]{1,0:T(8,128)(2,1)}, bf16[112,1024]{1,0:T(8,128)(2,1)S(1)}, u32[]{:S(2)}, u32[]{:S(2)}) collective-permute-start(bf16[112,1024]{1,0:T(8,128)(2,1)} %get-tuple-element.168.refs_0_), channel_id=1, source_target_pairs={{0,4},{4,8},{8,12},{12,16},{16,20},{20,24},{24,28},{28,0},{1,5},{5... | collective-permute-start | bytes 688136 | tf_op jit(solution)/shard_map/ppermute | solution.py:31
  48.4 22.9 %copy-start.18 = (bf16[112,1024]{1,0:T(8,128)(2,1)}, bf16[112,1024]{1,0:T(8,128)(2,1)S(1)}, u32[]{:S(2)}) copy-start(bf16[112,1024]{1,0:T(8,128)(2,1)S(1)} %collective-permute-done.13.refs_1_) | copy-start | bytes 688132
  48.4 6.4 %collective-permute-start.14 = (bf16[112,1024]{1,0:T(8,128)(2,1)S(1)}, bf16[112,1024]{1,0:T(8,128)(2,1)S(1)}, u32[]{:S(2)}, u32[]{:S(2)}) collective-permute-start(bf16[112,1024]{1,0:T(8,128)(2,1)S(1)} %collective-permute-done.13.refs_1_), channel_id=1, source_target_pairs={{0,28},{4,0},{8,4},{12,8},{16,12},{20,16},{24,20},{28,24},{1,29},{... | collective-permute-start | bytes 688136 | tf_op jit(solution)/shard_map/ppermute | solution.py:31
  51.3 20.0 %copy-start.19 = (bf16[112,1024]{1,0:T(8,128)(2,1)}, bf16[112,1024]{1,0:T(8,128)(2,1)S(1)}, u32[]{:S(2)}) copy-start(bf16[112,1024]{1,0:T(8,128)(2,1)S(1)} %collective-permute-done.16.refs_8_) | copy-start | bytes 688132
  51.4 6.2 %collective-permute-start.17 = (bf16[112,1024]{1,0:T(8,128)(2,1)S(1)}, bf16[112,1024]{1,0:T(8,128)(2,1)S(1)}, u32[]{:S(2)}, u32[]{:S(2)}) collective-permute-start(bf16[112,1024]{1,0:T(8,128)(2,1)S(1)} %collective-permute-done.16.refs_8_), channel_id=1, source_target_pairs={{0,4},{4,8},{8,12},{12,16},{16,20},{20,24},{24,28},{28,0},{1,5},{5... | collective-permute-start | bytes 688136 | tf_op jit(solution)/shard_map/ppermute | solution.py:31
  54.8 7.4 %collective-permute-start.15 = (bf16[112,1024]{1,0:T(8,128)(2,1)S(1)}, bf16[112,1024]{1,0:T(8,128)(2,1)S(1)}, u32[]{:S(2)}, u32[]{:S(2)}) collective-permute-start(bf16[112,1024]{1,0:T(8,128)(2,1)S(1)} %collective-permute-done.14.refs_2_), channel_id=1, source_target_pairs={{0,28},{4,0},{8,4},{12,8},{16,12},{20,16},{24,20},{28,24},{1,29},{... | collective-permute-start | bytes 688136 | tf_op jit(solution)/shard_map/ppermute | solution.py:31
  57.6 7.4 %collective-permute-start.18 = (bf16[112,1024]{1,0:T(8,128)(2,1)S(1)}, bf16[112,1024]{1,0:T(8,128)(2,1)S(1)}, u32[]{:S(2)}, u32[]{:S(2)}) collective-permute-start(bf16[112,1024]{1,0:T(8,128)(2,1)S(1)} %collective-permute-done.17.refs_7_), channel_id=1, source_target_pairs={{0,4},{4,8},{8,12},{12,16},{16,20},{20,24},{24,28},{28,0},{1,5},{5... | collective-permute-start | bytes 688136 | tf_op jit(solution)/shard_map/ppermute | solution.py:31
  62.2 9.2 %collective-permute-start.20 = (bf16[64,1024]{1,0:T(8,128)(2,1)S(1)}, bf16[64,1024]{1,0:T(8,128)(2,1)S(1)}, u32[]{:S(2)}, u32[]{:S(2)}) collective-permute-start(bf16[64,1024]{1,0:T(8,128)(2,1)S(1)} %slice.64), channel_id=1, source_target_pairs={{0,28},{4,0},{8,4},{12,8},{16,12},{20,16},{24,20},{28,24},{1,29},{... | collective-permute-start | bytes 393224 | tf_op jit(solution)/shard_map/ppermute | solution.py:31
  65.0 6.4 %collective-permute-start.19 = (bf16[48,1024]{1,0:T(8,128)(2,1)S(1)}, bf16[48,1024]{1,0:T(8,128)(2,1)S(1)}, u32[]{:S(2)}, u32[]{:S(2)}) collective-permute-start(bf16[48,1024]{1,0:T(8,128)(2,1)S(1)} %slice.63), channel_id=1, source_target_pairs={{0,4},{4,8},{8,12},{12,16},{16,20},{20,24},{24,28},{28,0},{1,5},{5... | collective-permute-start | bytes 294920 | tf_op jit(solution)/shard_map/ppermute | solution.py:31
  78.7 9.7 %collective-permute-start.21 = (bf16[2,128,1152]{2,1,0:T(8,128)(2,1)}, bf16[2,128,1152]{2,1,0:T(8,128)(2,1)S(1)}, u32[]{:S(2)}, u32[]{:S(2)}) collective-permute-start(bf16[2,128,1152]{2,1,0:T(8,128)(2,1)} %get-tuple-element.176), channel_id=1, source_target_pairs={{0,1},{1,0},{2,3},{3,2},{4,5},{5,4},{6,7},{7,6},{8,9},{9,8},{10,11... | collective-permute-start | bytes 1769480 | tf_op jit(solution)/shard_map/ppermute | solution.py:31
  89.8 19.0 %copy-start.2 = (bf16[2,128,1152]{2,1,0:T(8,128)(2,1)}, bf16[2,128,1152]{2,1,0:T(8,128)(2,1)S(1)}, u32[]{:S(2)}) copy-start(bf16[2,128,1152]{2,1,0:T(8,128)(2,1)S(1)} %add_convert_fusion.near_ref) | copy-start | bytes 1769476
  89.8 18.9 %collective-permute-start.22 = (bf16[2,128,1152]{2,1,0:T(8,128)(2,1)S(1)}, bf16[2,128,1152]{2,1,0:T(8,128)(2,1)S(1)}, u32[]{:S(2)}, u32[]{:S(2)}) collective-permute-start(bf16[2,128,1152]{2,1,0:T(8,128)(2,1)S(1)} %add_convert_fusion.near_ref), channel_id=1, source_target_pairs={{0,2},{2,0},{1,3},{3,1},{4,6},{6,4},{5,7},{7,5},{8,10},{10,8},{9,1... | collective-permute-start | bytes 1769480 | tf_op jit(solution)/shard_map/ppermute | solution.py:31
  91.1 6.6 %collective-permute-start.23 = (bf16[64,1024]{1,0:T(8,128)(2,1)S(1)}, bf16[64,1024]{1,0:T(8,128)(2,1)S(1)}, u32[]{:S(2)}, u32[]{:S(2)}) collective-permute-start(bf16[64,1024]{1,0:T(8,128)(2,1)S(1)} %bitcast.46), channel_id=1, source_target_pairs={{0,0},{1,4},{2,8},{3,12},{16,16},{17,20},{24,24},{25,28},{4,1},{5,... | collective-permute-start | bytes 393224 | tf_op jit(solution)/shard_map/ppermute | solution.py:478
  93.1 9.9 %collective-permute-start.24 = (bf16[32,1024]{1,0:T(8,128)(2,1)S(1)}, bf16[32,1024]{1,0:T(8,128)(2,1)S(1)}, u32[]{:S(2)}, u32[]{:S(2)}) collective-permute-start(bf16[32,1024]{1,0:T(8,128)(2,1)S(1)} %bitcast.47), channel_id=1, source_target_pairs={{0,0},{1,4},{2,8},{3,12},{4,16},{5,20},{6,24},{7,28},{8,1},{9,5},{... | collective-permute-start | bytes 196616 | tf_op jit(solution)/shard_map/ppermute | solution.py:479
  103.0 27.9 %copy-start.8 = (bf16[96,1024]{1,0:T(8,128)(2,1)}, bf16[96,1024]{1,0:T(8,128)(2,1)S(1)}, u32[]{:S(2)}) copy-start(bf16[96,1024]{1,0:T(8,128)(2,1)S(1)} %constant_dynamic-update-slice_fusion.refs_0_.refs_1_) | copy-start | bytes 589828
  103.0 9.3 %collective-permute-start.26 = (bf16[96,1024]{1,0:T(8,128)(2,1)S(1)}, bf16[96,1024]{1,0:T(8,128)(2,1)S(1)}, u32[]{:S(2)}, u32[]{:S(2)}) collective-permute-start(bf16[96,1024]{1,0:T(8,128)(2,1)S(1)} %constant_dynamic-update-slice_fusion.refs_0_.refs_1_), channel_id=1, source_target_pairs={{0,4},{4,8},{8,12},{12,16},{16,20},{20,24},{24,28},{28,0},{1,5},{5... | collective-permute-start | bytes 589832 | tf_op jit(solution)/shard_map/ppermute | solution.py:31
  103.1 9.4 %collective-permute-start.25 = (bf16[96,1024]{1,0:T(8,128)(2,1)S(1)}, bf16[96,1024]{1,0:T(8,128)(2,1)S(1)}, u32[]{:S(2)}, u32[]{:S(2)}) collective-permute-start(bf16[96,1024]{1,0:T(8,128)(2,1)S(1)} %constant_dynamic-update-slice_fusion.refs_0_.refs_1_), channel_id=1, source_target_pairs={{0,28},{4,0},{8,4},{12,8},{16,12},{20,16},{24,20},{28,24},{1,29},{... | collective-permute-start | bytes 589832 | tf_op jit(solution)/shard_map/ppermute | solution.py:31
  112.3 18.6 %collective-permute-start.33 = (bf16[2,128,1024]{2,1,0:T(8,128)(2,1)}, bf16[2,128,1024]{2,1,0:T(8,128)(2,1)S(1)}, u32[]{:S(2)}, u32[]{:S(2)}) collective-permute-start(bf16[2,128,1024]{2,1,0:T(8,128)(2,1)} %get-tuple-element.181.refs_9_), channel_id=1, source_target_pairs={{0,1},{1,0},{2,3},{3,2},{4,5},{5,4},{6,7},{7,6},{8,9},{9,8},{10,11... | collective-permute-start | bytes 1572872 | tf_op jit(solution)/shard_map/ppermute | solution.py:31
  112.3 7.3 %collective-permute-start.27 = (bf16[96,1024]{1,0:T(8,128)(2,1)S(1)}, bf16[96,1024]{1,0:T(8,128)(2,1)S(1)}, u32[]{:S(2)}, u32[]{:S(2)}) collective-permute-start(bf16[96,1024]{1,0:T(8,128)(2,1)S(1)} %collective-permute-done.26.refs_8_.refs_9_), channel_id=1, source_target_pairs={{0,4},{4,8},{8,12},{12,16},{16,20},{20,24},{24,28},{28,0},{1,5},{5... | collective-permute-start | bytes 589832 | tf_op jit(solution)/shard_map/ppermute | solution.py:31
  112.5 7.1 %collective-permute-start.28 = (bf16[96,1024]{1,0:T(8,128)(2,1)S(1)}, bf16[96,1024]{1,0:T(8,128)(2,1)S(1)}, u32[]{:S(2)}, u32[]{:S(2)}) collective-permute-start(bf16[96,1024]{1,0:T(8,128)(2,1)S(1)} %collective-permute-done.25.refs_1_.refs_2_), channel_id=1, source_target_pairs={{0,28},{4,0},{8,4},{12,8},{16,12},{20,16},{24,20},{28,24},{1,29},{... | collective-permute-start | bytes 589832 | tf_op jit(solution)/shard_map/ppermute | solution.py:31
  119.7 6.5 %collective-permute-start.30 = (bf16[96,1024]{1,0:T(8,128)(2,1)S(1)}, bf16[96,1024]{1,0:T(8,128)(2,1)S(1)}, u32[]{:S(2)}, u32[]{:S(2)}) collective-permute-start(bf16[96,1024]{1,0:T(8,128)(2,1)S(1)} %collective-permute-done.27.refs_7_.refs_8_), channel_id=1, source_target_pairs={{0,4},{4,8},{8,12},{12,16},{16,20},{20,24},{24,28},{28,0},{1,5},{5... | collective-permute-start | bytes 589832 | tf_op jit(solution)/shard_map/ppermute | solution.py:31
  120.2 6.0 %collective-permute-start.29 = (bf16[96,1024]{1,0:T(8,128)(2,1)S(1)}, bf16[96,1024]{1,0:T(8,128)(2,1)S(1)}, u32[]{:S(2)}, u32[]{:S(2)}) collective-permute-start(bf16[96,1024]{1,0:T(8,128)(2,1)S(1)} %collective-permute-done.28.refs_2_.refs_3_), channel_id=1, source_target_pairs={{0,28},{4,0},{8,4},{12,8},{16,12},{20,16},{24,20},{28,24},{1,29},{... | collective-permute-start | bytes 589832 | tf_op jit(solution)/shard_map/ppermute | solution.py:31
  126.1 4.8 %collective-permute-start.31 = (bf16[48,1024]{1,0:T(8,128)(2,1)S(1)}, bf16[48,1024]{1,0:T(8,128)(2,1)S(1)}, u32[]{:S(2)}, u32[]{:S(2)}) collective-permute-start(bf16[48,1024]{1,0:T(8,128)(2,1)S(1)} %slice.65), channel_id=1, source_target_pairs={{0,4},{4,8},{8,12},{12,16},{16,20},{20,24},{24,28},{28,0},{1,5},{5... | collective-permute-start | bytes 294920 | tf_op jit(solution)/shard_map/ppermute | solution.py:31
  126.3 4.6 %collective-permute-start.32 = (bf16[48,1024]{1,0:T(8,128)(2,1)S(1)}, bf16[48,1024]{1,0:T(8,128)(2,1)S(1)}, u32[]{:S(2)}, u32[]{:S(2)}) collective-permute-start(bf16[48,1024]{1,0:T(8,128)(2,1)S(1)} %slice.66), channel_id=1, source_target_pairs={{0,28},{4,0},{8,4},{12,8},{16,12},{20,16},{24,20},{28,24},{1,29},{... | collective-permute-start | bytes 294920 | tf_op jit(solution)/shard_map/ppermute | solution.py:31
  137.5 7.1 %collective-permute-start = (bf16[512,256]{1,0:T(8,128)(2,1)S(1)}, bf16[512,256]{1,0:T(8,128)(2,1)S(1)}, u32[]{:S(2)}, u32[]{:S(2)}) collective-permute-start(bf16[512,256]{1,0:T(8,128)(2,1)S(1)} %copy.28.up_ref), channel_id=1, source_target_pairs={{0,4},{4,8},{8,12},{12,16},{16,20},{20,24},{24,28},{28,0},{1,5},{5... | collective-permute-start | bytes 786440 | tf_op jit(solution)/shard_map/while/body/eval_jaxpr/ppermute | solution.py:31
  138.2 6.3 %collective-permute-start.1 = (bf16[512,256]{1,0:T(8,128)(2,1)S(1)}, bf16[512,256]{1,0:T(8,128)(2,1)S(1)}, u32[]{:S(2)}, u32[]{:S(2)}) collective-permute-start(bf16[512,256]{1,0:T(8,128)(2,1)S(1)} %copy.29.down_ref), channel_id=1, source_target_pairs={{0,28},{4,0},{8,4},{12,8},{16,12},{20,16},{24,20},{28,24},{1,29},{... | collective-permute-start | bytes 786440 | tf_op jit(solution)/shard_map/while/body/eval_jaxpr/ppermute | solution.py:31
  144.6 6.5 %collective-permute-start = (bf16[512,256]{1,0:T(8,128)(2,1)S(1)}, bf16[512,256]{1,0:T(8,128)(2,1)S(1)}, u32[]{:S(2)}, u32[]{:S(2)}) collective-permute-start(bf16[512,256]{1,0:T(8,128)(2,1)S(1)} %copy.28.up_ref), channel_id=1, source_target_pairs={{0,4},{4,8},{8,12},{12,16},{16,20},{20,24},{24,28},{28,0},{1,5},{5... | collective-permute-start | bytes 786440 | tf_op jit(solution)/shard_map/while/body/eval_jaxpr/ppermute | solution.py:31
  146.4 5.3 %collective-permute-start.1 = (bf16[512,256]{1,0:T(8,128)(2,1)S(1)}, bf16[512,256]{1,0:T(8,128)(2,1)S(1)}, u32[]{:S(2)}, u32[]{:S(2)}) collective-permute-start(bf16[512,256]{1,0:T(8,128)(2,1)S(1)} %copy.29.down_ref), channel_id=1, source_target_pairs={{0,28},{4,0},{8,4},{12,8},{16,12},{20,16},{24,20},{28,24},{1,29},{... | collective-permute-start | bytes 786440 | tf_op jit(solution)/shard_map/while/body/eval_jaxpr/ppermute | solution.py:31
  151.7 6.7 %collective-permute-start = (bf16[512,256]{1,0:T(8,128)(2,1)S(1)}, bf16[512,256]{1,0:T(8,128)(2,1)S(1)}, u32[]{:S(2)}, u32[]{:S(2)}) collective-permute-start(bf16[512,256]{1,0:T(8,128)(2,1)S(1)} %copy.28.up_ref), channel_id=1, source_target_pairs={{0,4},{4,8},{8,12},{12,16},{16,20},{20,24},{24,28},{28,0},{1,5},{5... | collective-permute-start | bytes 786440 | tf_op jit(solution)/shard_map/while/body/eval_jaxpr/ppermute | solution.py:31
  153.6 5.5 %collective-permute-start.1 = (bf16[512,256]{1,0:T(8,128)(2,1)S(1)}, bf16[512,256]{1,0:T(8,128)(2,1)S(1)}, u32[]{:S(2)}, u32[]{:S(2)}) collective-permute-start(bf16[512,256]{1,0:T(8,128)(2,1)S(1)} %copy.29.down_ref), channel_id=1, source_target_pairs={{0,28},{4,0},{8,4},{12,8},{16,12},{20,16},{24,20},{28,24},{1,29},{... | collective-permute-start | bytes 786440 | tf_op jit(solution)/shard_map/while/body/eval_jaxpr/ppermute | solution.py:31
  159.1 7.8 %collective-permute-start = (bf16[512,256]{1,0:T(8,128)(2,1)S(1)}, bf16[512,256]{1,0:T(8,128)(2,1)S(1)}, u32[]{:S(2)}, u32[]{:S(2)}) collective-permute-start(bf16[512,256]{1,0:T(8,128)(2,1)S(1)} %copy.28.up_ref), channel_id=1, source_target_pairs={{0,4},{4,8},{8,12},{12,16},{16,20},{20,24},{24,28},{28,0},{1,5},{5... | collective-permute-start | bytes 786440 | tf_op jit(solution)/shard_map/while/body/eval_jaxpr/ppermute | solution.py:31
  160.9 7.8 %collective-permute-start.1 = (bf16[512,256]{1,0:T(8,128)(2,1)S(1)}, bf16[512,256]{1,0:T(8,128)(2,1)S(1)}, u32[]{:S(2)}, u32[]{:S(2)}) collective-permute-start(bf16[512,256]{1,0:T(8,128)(2,1)S(1)} %copy.29.down_ref), channel_id=1, source_target_pairs={{0,28},{4,0},{8,4},{12,8},{16,12},{20,16},{24,20},{28,24},{1,29},{... | collective-permute-start | bytes 786440 | tf_op jit(solution)/shard_map/while/body/eval_jaxpr/ppermute | solution.py:31
  172.6 9.9 %collective-permute-start.34 = (bf16[2,128,1024]{2,1,0:T(8,128)(2,1)}, bf16[2,128,1024]{2,1,0:T(8,128)(2,1)S(1)}, u32[]{:S(2)}, u32[]{:S(2)}) collective-permute-start(bf16[2,128,1024]{2,1,0:T(8,128)(2,1)} %get-tuple-element.189), channel_id=1, source_target_pairs={{0,1},{1,0},{2,3},{3,2},{4,5},{5,4},{6,7},{7,6},{8,9},{9,8},{10,11... | collective-permute-start | bytes 1572872 | tf_op jit(solution)/shard_map/ppermute | solution.py:31
  182.9 11.2 %collective-permute-start.35 = (bf16[128,1024]{1,0:T(8,128)(2,1)S(1)}, bf16[128,1024]{1,0:T(8,128)(2,1)S(1)}, u32[]{:S(2)}, u32[]{:S(2)}) collective-permute-start(bf16[128,1024]{1,0:T(8,128)(2,1)S(1)} %fusion.3), channel_id=1, source_target_pairs={{0,32},{1,33},{2,34},{3,35},{32,64},{33,65},{34,66},{35,67},{64,96... | collective-permute-start | bytes 786440 | tf_op jit(solution)/shard_map/ppermute | solution.py:548
  183.0 17.5 %collective-permute-start.36 = (bf16[128,1024]{1,0:T(8,128)(2,1)S(1)}, bf16[128,1024]{1,0:T(8,128)(2,1)S(1)}, u32[]{:S(2)}, u32[]{:S(2)}) collective-permute-start(bf16[128,1024]{1,0:T(8,128)(2,1)S(1)} %fusion.6), channel_id=1, source_target_pairs={{0,34},{1,35},{2,32},{3,33},{32,66},{33,67},{34,64},{35,65},{64,98... | collective-permute-start | bytes 786440 | tf_op jit(solution)/shard_map/ppermute | solution.py:549
  (45 other events, 305.4 us)
